TPU v7x, 32 devices: a whole 2x2x4 slice. The times are simulated.
32 devices in a mesh: seq: 4 (over x, core), clip: 8 (over z, y).
Axes of the slice: x: 2, y: 2, z: 4, core: 2. Of those that a mesh axis runs over, the one named last changes fastest.
Arguments:
- x_vis: bfloat16 [24, 157, 768], P('clip'), may hold values from -6 to 6
- vis_pos: int32 [24, 157], P('clip'), may hold values from 0 to 1567, as said below
- w_proj: bfloat16 [768, 384], replicated, may hold values from -0.21875 to 0.21875
- b_proj: float32 [384], replicated, may hold values from -3 to 3
- mask_token: float32 [384], replicated, may hold values from -4 to 4
- ln1_gain: float32 [384], replicated, may hold values from 0.25 to 1.75
- ln1_bias: float32 [384], replicated, may hold values from -2 to 2
- w_qkv: bfloat16 [384, 1152], replicated, may hold values from -0.3125 to 0.3125
- q_bias: float32 [384], replicated, may hold values from -2 to 2
- v_bias: float32 [384], replicated, may hold values from -3 to 3
- w_out: bfloat16 [384, 384], replicated, may hold values from -4 to 4
- b_out: float32 [384], replicated, may hold values from -2 to 2
- ln2_gain: float32 [384], replicated, may hold values from 0.25 to 1.75
- ln2_bias: float32 [384], replicated, may hold values from -2 to 2
- w_fc1: bfloat16 [384, 1536], replicated, may hold values from -0.3125 to 0.3125
- b_fc1: float32 [1536], replicated, may hold values from -3 to 3
- w_fc2: bfloat16 [1536, 384], replicated, may hold values from -0.15625 to 0.15625
- b_fc2: float32 [384], replicated, may hold values from -2 to 2
- cotangent: bfloat16 [24, 1568, 384], P('clip', 'seq'), may hold values from -6 to 6
Outputs:
- output: bfloat16 [24, 1568, 384], P('clip', 'seq')
- grad_x: float32 [24, 157, 768], P('clip')
- grad_w_proj: float32 [768, 384], replicated
- grad_b_proj: float32 [384], replicated
- grad_mask: float32 [384], replicated
- grad_ln1_gain: float32 [384], replicated
- grad_ln1_bias: float32 [384], replicated
- grad_w_qkv: float32 [384, 1152], replicated
- grad_q_bias: float32 [384], replicated
- grad_v_bias: float32 [384], replicated
- grad_w_out: float32 [384, 384], replicated
- grad_b_out: float32 [384], replicated
- grad_ln2_gain: float32 [384], replicated
- grad_ln2_bias: float32 [384], replicated
- grad_w_fc1: float32 [384, 1536], replicated
- grad_b_fc1: float32 [1536], replicated
- grad_w_fc2: float32 [1536, 384], replicated
- grad_b_fc2: float32 [384], replicated
- trust: float32 [4], replicated
- trust_qkv: float32 [1], replicated
Inputs may be any that keep to these rules, and one draw needn't show every extreme that they name: `vis_pos`: each clip's 157 visible positions, in rising order, all different.
All inputs are finite; a program needn't handle non-finite values.
Results may differ from a plain program's by a relative error of at most 0.01.
Values may be sent and summed in bfloat16 or wider, within the bound.
No kernel may reach another device: no remote copies, remote signals or barrier semaphores. Data moves between devices by JAX's collectives and lax.ppermute only.
A program may use at most 256 MiB of HBM per device.

v0:
```python
import math

import jax
import jax.numpy as jnp
from jax import lax
from jax.sharding import PartitionSpec as P

D = 384
HEADS = 6
HEAD = 64
LEN = 1568


exact_prec = lax.Precision.HIGHEST


def sinusoid(length, columns):
    positions = jnp.arange(length, dtype=jnp.float32)[:, None]
    column = jnp.arange(columns, dtype=jnp.int32)
    exponent = (2 * (column // 2)).astype(jnp.float32) / columns
    angles = positions / jnp.power(10000.0, exponent)[None, :]
    return jnp.where((column % 2)[None, :] == 0, jnp.sin(angles), jnp.cos(angles))


def layer_norm(inputs, gain_vec, shift_vec):
    average = jnp.mean(inputs, axis=-1, keepdims=True)
    centered = inputs - average
    variance = jnp.mean(centered * centered, axis=-1, keepdims=True)
    return centered * lax.rsqrt(variance + 1e-05) * gain_vec + shift_vec


def gelu_exact(values):
    return jax.nn.gelu(values, approximate=False)


def shards(
    x_vis,
    vis_pos,
    w_proj,
    b_proj,
    mask_token,
    ln1_gain,
    ln1_bias,
    w_qkv,
    q_bias,
    v_bias,
    w_out,
    b_out,
    ln2_gain,
    ln2_bias,
    w_fc1,
    b_fc1,
    w_fc2,
    b_fc2,
    cotangent,
):
    row_count = LEN // lax.axis_size("seq")
    score_scale = HEAD ** (-0.5)
    first_row = lax.axis_index("seq") * row_count
    projected = (
        jnp.einsum("cvi,id->cvd", x_vis, w_proj, preferred_element_type=jnp.float32) + b_proj
    )
    places = first_row + lax.iota(jnp.int32, row_count)
    onehot = (vis_pos[:, None, :] == places[None, :, None]).astype(jnp.float32)
    visible = jnp.sum(onehot, axis=2, keepdims=True)
    position_table = lax.dynamic_slice_in_dim(sinusoid(LEN, D), first_row, row_count, 0)
    embedded = (
        jnp.einsum("crv,cvd->crd", onehot, projected, precision=exact_prec)
        + (1.0 - visible) * mask_token
        + position_table
    )
    normed = layer_norm(embedded, ln1_gain, ln1_bias).astype(jnp.bfloat16)
    qkv_mixed = jnp.einsum("crd,de->cre", normed, w_qkv, preferred_element_type=jnp.float32)
    queries = (qkv_mixed[..., :D] + q_bias).astype(jnp.bfloat16)
    keys_local = qkv_mixed[..., D : 2 * D].astype(jnp.bfloat16)
    values_local = (qkv_mixed[..., 2 * D :] + v_bias).astype(jnp.bfloat16)
    keys_all, values_all = (
        lax.all_gather(keys_local, "seq", axis=1, tiled=True),
        lax.all_gather(values_local, "seq", axis=1, tiled=True),
    )

    def attend(sliced):
        query_one, key_one, value_one = sliced
        q_heads = query_one.reshape(row_count, HEADS, HEAD)
        k_heads = key_one.reshape(LEN, HEADS, HEAD)
        v_heads = value_one.reshape(LEN, HEADS, HEAD)
        scores = (
            jnp.einsum("qhe,khe->hqk", q_heads, k_heads, preferred_element_type=jnp.float32)
            * score_scale
        )
        largest = jnp.max(scores, axis=-1, keepdims=True)
        exponent = jnp.exp(scores - largest)
        totals = jnp.sum(exponent, axis=-1, keepdims=True)
        attn_probs = (exponent / totals).astype(jnp.bfloat16)
        attended = jnp.einsum(
            "hqk,khe->qhe", attn_probs, v_heads, preferred_element_type=jnp.float32
        )
        return (attended.reshape(row_count, D).astype(jnp.bfloat16), largest + jnp.log(totals))

    attended, log_totals = lax.map(attend, (queries, keys_all, values_all))
    branch = jnp.einsum("crd,de->cre", attended, w_out, preferred_element_type=jnp.float32) + b_out
    middle = embedded + branch
    normed2 = layer_norm(middle, ln2_gain, ln2_bias).astype(jnp.bfloat16)
    hidden_pre = (
        jnp.einsum("crd,df->crf", normed2, w_fc1, preferred_element_type=jnp.float32) + b_fc1
    )
    hidden = gelu_exact(hidden_pre).astype(jnp.bfloat16)
    output = (
        middle
        + jnp.einsum("crf,fd->crd", hidden, w_fc2, preferred_element_type=jnp.float32)
        + b_fc2
    ).astype(jnp.bfloat16)
    grad_out_f = cotangent.astype(jnp.float32)
    grad_w_fc2 = jnp.einsum("crf,crd->fd", hidden, cotangent, preferred_element_type=jnp.float32)
    grad_b_fc2 = jnp.sum(grad_out_f, axis=(0, 1))
    grad_hidden = jnp.einsum("crd,fd->crf", cotangent, w_fc2, preferred_element_type=jnp.float32)
    unused_gelu, pull_gelu = jax.vjp(gelu_exact, hidden_pre)
    grad_pre = pull_gelu(grad_hidden)[0].astype(jnp.bfloat16)
    grad_w_fc1 = jnp.einsum("crd,crf->df", normed2, grad_pre, preferred_element_type=jnp.float32)
    grad_b_fc1 = jnp.sum(grad_pre.astype(jnp.float32), axis=(0, 1))
    grad_normed2 = jnp.einsum("crf,df->crd", grad_pre, w_fc1, preferred_element_type=jnp.float32)
    unused_norm2, pull_norm2 = jax.vjp(layer_norm, middle, ln2_gain, ln2_bias)
    grad_mid_ln, grad_ln2_gain, grad_ln2_bias = pull_norm2(grad_normed2)
    grad_middle = grad_out_f + grad_mid_ln
    grad_branch = grad_middle.astype(jnp.bfloat16)
    grad_w_out = jnp.einsum(
        "crd,cre->de", attended, grad_branch, preferred_element_type=jnp.float32
    )
    grad_b_out = jnp.sum(grad_branch.astype(jnp.float32), axis=(0, 1))
    grad_attended = jnp.einsum(
        "cre,de->crd", grad_branch, w_out, preferred_element_type=jnp.float32
    ).astype(jnp.bfloat16)

    def attend_back(sliced):
        query_one, key_one, value_one, grad_one, logtot_one = sliced
        q_heads = query_one.reshape(row_count, HEADS, HEAD)
        k_heads = key_one.reshape(LEN, HEADS, HEAD)
        v_heads = value_one.reshape(LEN, HEADS, HEAD)
        g_heads = grad_one.reshape(row_count, HEADS, HEAD)
        scores = (
            jnp.einsum("qhe,khe->hqk", q_heads, k_heads, preferred_element_type=jnp.float32)
            * score_scale
        )
        attn_probs = jnp.exp(scores - logtot_one)
        grad_probs = jnp.einsum(
            "qhe,khe->hqk", g_heads, v_heads, preferred_element_type=jnp.float32
        )
        row_inner = jnp.sum(grad_probs * attn_probs, axis=-1, keepdims=True)
        grad_scores = (attn_probs * (grad_probs - row_inner)).astype(jnp.bfloat16)
        grad_query = (
            jnp.einsum(
                "hqk,khe->qhe", grad_scores, k_heads, preferred_element_type=jnp.float32
            ).reshape(row_count, D)
            * score_scale
        )
        grad_key = (
            jnp.einsum(
                "hqk,qhe->khe", grad_scores, q_heads, preferred_element_type=jnp.float32
            ).reshape(LEN, D)
            * score_scale
        )
        grad_value = jnp.einsum(
            "hqk,qhe->khe",
            attn_probs.astype(jnp.bfloat16),
            g_heads,
            preferred_element_type=jnp.float32,
        ).reshape(LEN, D)
        return (grad_query, grad_key, grad_value)

    grad_query, grad_key_part, grad_value_part = lax.map(
        attend_back, (queries, keys_all, values_all, grad_attended, log_totals)
    )
    grad_keys, grad_values = (
        lax.psum_scatter(grad_key_part, "seq", scatter_dimension=1, tiled=True),
        lax.psum_scatter(grad_value_part, "seq", scatter_dimension=1, tiled=True),
    )
    grad_qkv = jnp.concatenate(
        [
            grad_query.astype(jnp.bfloat16),
            grad_keys.astype(jnp.bfloat16),
            grad_values.astype(jnp.bfloat16),
        ],
        axis=-1,
    )
    grad_q_bias = jnp.sum(grad_qkv[..., :D].astype(jnp.float32), axis=(0, 1))
    grad_v_bias = jnp.sum(grad_qkv[..., 2 * D :].astype(jnp.float32), axis=(0, 1))
    grad_w_qkv = jnp.einsum("crd,cre->de", normed, grad_qkv, preferred_element_type=jnp.float32)
    grad_normed = jnp.einsum("cre,de->crd", grad_qkv, w_qkv, preferred_element_type=jnp.float32)
    unused_norm1, pull_norm1 = jax.vjp(layer_norm, embedded, ln1_gain, ln1_bias)
    grad_emb_ln, grad_ln1_gain, grad_ln1_bias = pull_norm1(grad_normed)
    grad_embedded = grad_middle + grad_emb_ln
    grad_mask = jnp.sum(grad_embedded * (1.0 - visible), axis=(0, 1))
    grad_proj_part = jnp.einsum("crv,crd->cvd", onehot, grad_embedded, precision=exact_prec)
    grad_projected = lax.psum(grad_proj_part.astype(jnp.bfloat16), "seq")
    grad_x = jnp.einsum("cvd,id->cvi", grad_projected, w_proj, preferred_element_type=jnp.float32)
    leading = (lax.axis_index("seq") == 0).astype(jnp.float32)
    grad_w_proj = (
        jnp.einsum("cvi,cvd->id", x_vis, grad_projected, preferred_element_type=jnp.float32)
        * leading
    )
    grad_b_proj = jnp.sum(grad_projected.astype(jnp.float32), axis=(0, 1)) * leading
    grad_list = [
        grad_w_proj,
        grad_b_proj,
        grad_mask,
        grad_ln1_gain,
        grad_ln1_bias,
        grad_w_qkv,
        grad_q_bias,
        grad_v_bias,
        grad_w_out,
        grad_b_out,
        grad_ln2_gain,
        grad_ln2_bias,
        grad_w_fc1,
        grad_b_fc1,
        grad_w_fc2,
        grad_b_fc2,
    ]
    offsets = []
    running = 0
    for tensor in grad_list:
        offsets.append(running)
        running += math.prod(tensor.shape)
    flat = jnp.concatenate([tensor.reshape(-1) for tensor in grad_list])
    matrix_slots = [0, 5, 8, 12, 14]
    matrix_list = [w_proj, w_qkv, w_out, w_fc1, w_fc2]
    counts_list = [math.prod(grad_list[slot].shape) for slot in matrix_slots]
    summed = lax.psum(flat, ("seq", "clip"))
    squares = jnp.stack(
        [
            jnp.sum(summed[offsets[slot] : offsets[slot] + counts_list[number]] ** 2)
            for number, slot in enumerate(matrix_slots)
        ]
    )
    results = [
        summed[offsets[number] : offsets[number] + math.prod(tensor.shape)].reshape(tensor.shape)
        for number, tensor in enumerate(grad_list)
    ]
    trust_all = jnp.stack(
        [
            jnp.sqrt(jnp.mean(matrix.astype(jnp.float32) ** 2))
            / jnp.sqrt(squares[number] / counts_list[number] + 1e-06)
            for number, matrix in enumerate(matrix_list)
        ]
    )
    trust = jnp.concatenate([trust_all[:1], trust_all[2:]])
    trust_qkv = trust_all[1:2]
    return (
        output,
        grad_x,
        results[0],
        results[1],
        results[2],
        results[3],
        results[4],
        results[5],
        results[6],
        results[7],
        results[8],
        results[9],
        results[10],
        results[11],
        results[12],
        results[13],
        results[14],
        results[15],
        trust,
        trust_qkv,
    )


def solution(mesh):
    return jax.shard_map(
        shards,
        mesh=mesh,
        in_specs=(
            P("clip", None, None),
            P("clip", None),
            P(),
            P(),
            P(),
            P(),
            P(),
            P(),
            P(),
            P(),
            P(),
            P(),
            P(),
            P(),
            P(),
            P(),
            P(),
            P(),
            P("clip", "seq", None),
        ),
        out_specs=(
            P("clip", "seq", None),
            P("clip", None, None),
            P(),
            P(),
            P(),
            P(),
            P(),
            P(),
            P(),
            P(),
            P(),
            P(),
            P(),
            P(),
            P(),
            P(),
            P(),
            P(),
            P(),
            P(),
        ),
        check_vma=False,
    )
```

profile of v0, /device:TPU:1, one launch (start us, length us, event | category | flops | bytes accessed | tf_op | source)
XLA Modules:
  0.0 848.2 jit_solution(2511256565757544996)
XLA Ops:
  26.8 28.6 %all-gather.5.cloned.1.call-done = bf16[3,1568,384]{2,1,0:T(8,128)(2,1)} async-done(((bf16[3,392,384]{2,1,0:T(8,128)(2,1)}), bf16[3,1568,384]{2,1,0:T(8,128)(2,1)}) %all-gather.5.cloned.1.call-update) | async-done | bytes 3612688 | tf_op jit(solution)/shard_map/all_gather | solution.py:78
  61.6 27.0 %all-gather.3.cloned.1.call-done = bf16[3,1568,384]{2,1,0:T(8,128)(2,1)} async-done(((bf16[3,392,384]{2,1,0:T(8,128)(2,1)}), bf16[3,1568,384]{2,1,0:T(8,128)(2,1)}) %all-gather.3.cloned.1.call-update) | async-done | bytes 3612688 | tf_op jit(solution)/shard_map/all_gather | solution.py:79
  95.0 81.8 %while.26 = (s32[]{:T(128)}, bf16[3,392,384]{1,2,0:T(8,128)(2,1)}, f32[3,6,392,1]{2,1,3,0:T(8,128)S(1)}, bf16[3,1568,384]{1,2,0:T(8,128)(2,1)}, bf16[3,392,384]{...) while((s32[]{:T(128)}, bf16[3,392,384]{1,2,0:T(8,128)(2,1)}, f32[3,6,392,1]{2,1,3,0:T(8,128)S(1)}, ...), condition=%wide.region_6.7_spmd, body=%wide.region_3.6_spmd.sunk | while | flops 977451200 | bytes 53475364 | solution.py:100
  98.1 7.9 multiply_reduce_fusion.21
  106.0 8.2 fusion.120
  125.1 7.9 multiply_reduce_fusion.21
  133.0 8.2 fusion.120
  152.2 7.9 multiply_reduce_fusion.21
  160.1 8.2 fusion.120
  183.6 17.4 %multiply_convert_fusion.1 = (bf16[3,392,1536]{2,1,0:T(8,128)(2,1)}, f32[3,392,1536]{2,1,0:T(8,128)S(1)}) fusion(f32[3,392,1536]{2,1,0:T(8,128)S(1)} %get-tuple-element.221, f32[1536]{0:T(1024)S(1)} %copy-done.55, u8[392,1536]{1,0:T(8,128)(4,1)S(1)} %get-tuple-element.140, u8[392,1536]{1,0:T(8,128)(4,1)S(1)} %get-tuple-element.139), kind=kLoop, calls=%fused_computation.39 | loop fusion | flops 128249856 | bytes 19273728 | tf_op jit(solution)/shard_map/convert_element_type | solution.py:107
  213.8 159.5 %while.27 = (s32[]{:T(128)}, bf16[3,392,384]{2,1,0:T(8,128)(2,1)}, f32[3,1568,384]{2,1,0:T(8,128)}, f32[3,1568,384]{2,1,0:T(8,128)}, bf16[3,1568,384]{1,2,0:T(8,...) while((s32[]{:T(128)}, bf16[3,392,384]{2,1,0:T(8,128)(2,1)}, ...), condition=%wide.region_13.14_spmd, body=%wide.region_11.13_spmd.sunk | while | flops 2405435136 | bytes 276586112 | solution.py:170
  231.0 14.4 %multiply_reduce_fusion.22 = (f32[6,392]{1,0:T(8,128)S(1)}, f32[6,392,1568]{2,1,0:T(8,128)}) fusion(f32[6,392,1568]{2,1,0:T(8,128)} %copy-done.1, f32[6,392]{1,0:T(8,128)S(1)} %dynamic-slice_bitcast_fusion.2, bf16[392,6,64]{0,2,1:T(8,128)(2,1)} %bitcast.165, bf16[1568,6,64]{0,2,1:T(8,128)(2,1)S(1)} %bitcast.164), kind=kOutput, calls=%fused_computation.13.clone.1 | convolution fusion | flops 486805184 | bytes 31027584 | tf_op jit(solution)/shard_map/while/body/eval_jaxpr/qhe,khe->hqk/dot_general | solution.py:145
  245.8 7.6 multiply_convert_fusion.3
  284.1 14.4 %multiply_reduce_fusion.22 = (f32[6,392]{1,0:T(8,128)S(1)}, f32[6,392,1568]{2,1,0:T(8,128)}) fusion(f32[6,392,1568]{2,1,0:T(8,128)} %copy-done.1, f32[6,392]{1,0:T(8,128)S(1)} %dynamic-slice_bitcast_fusion.2, bf16[392,6,64]{0,2,1:T(8,128)(2,1)} %bitcast.165, bf16[1568,6,64]{0,2,1:T(8,128)(2,1)S(1)} %bitcast.164), kind=kOutput, calls=%fused_computation.13.clone.1 | convolution fusion | flops 486805184 | bytes 31027584 | tf_op jit(solution)/shard_map/while/body/eval_jaxpr/qhe,khe->hqk/dot_general | solution.py:145
  298.8 7.6 multiply_convert_fusion.3
  337.1 14.4 %multiply_reduce_fusion.22 = (f32[6,392]{1,0:T(8,128)S(1)}, f32[6,392,1568]{2,1,0:T(8,128)}) fusion(f32[6,392,1568]{2,1,0:T(8,128)} %copy-done.1, f32[6,392]{1,0:T(8,128)S(1)} %dynamic-slice_bitcast_fusion.2, bf16[392,6,64]{0,2,1:T(8,128)(2,1)} %bitcast.165, bf16[1568,6,64]{0,2,1:T(8,128)(2,1)S(1)} %bitcast.164), kind=kOutput, calls=%fused_computation.13.clone.1 | convolution fusion | flops 486805184 | bytes 31027584 | tf_op jit(solution)/shard_map/while/body/eval_jaxpr/qhe,khe->hqk/dot_general | solution.py:145
  351.9 7.6 multiply_convert_fusion.3
  399.8 38.0 %reduce-scatter.5.cloned.1.call-done = f32[3,392,384]{2,1,0:T(8,128)} async-done(((f32[3,1568,384]{2,1,0:T(8,128)}), f32[3,392,384]{2,1,0:T(8,128)}) %reduce-scatter.5.cloned.1.call-update) | async-done | bytes 1806352 | tf_op jit(solution)/shard_map/reduce_scatter | solution.py:175
  440.4 64.7 %reduce-scatter.3.cloned.1.call-done = f32[3,392,384]{2,1,0:T(8,128)} async-done(((f32[3,1568,384]{2,1,0:T(8,128)}), f32[3,392,384]{2,1,0:T(8,128)}) %reduce-scatter.3.cloned.1.call-update) | async-done | bytes 1806352 | tf_op jit(solution)/shard_map/reduce_scatter | solution.py:174
  522.0 24.7 %all-reduce.3.cloned.1.call-done = bf16[3,157,384]{2,1,0:T(8,128)(2,1)} async-done(((bf16[3,157,384]{2,1,0:T(8,128)(2,1)}), bf16[3,157,384]{2,1,0:T(8,128)(2,1)}) %all-reduce.3.cloned.1.call-update) | async-done | bytes 361744 | tf_op jit(solution)/shard_map/psum | solution.py:194
  562.0 15.5 %dynamic-update-slice.5 = f32[2069760]{0:T(1024)} dynamic-update-slice(f32[2069760]{0:T(1024)} %constant_dynamic-update-slice_fusion.12, f32[442368]{0:T(1024)S(1)} %reshape.290, s32[]{} %constant.199) | dynamic-update-slice | bytes 3538948
  586.3 21.3 %dynamic-update-slice.12 = f32[2069760]{0:T(1024)} dynamic-update-slice(f32[2069760]{0:T(1024)} %constant_dynamic-update-slice_fusion.6, f32[589824]{0:T(1024)} %reshape.292, s32[]{} %constant.206) | dynamic-update-slice | bytes 4718596
  608.9 20.1 %dynamic-update-slice.14 = f32[2069760]{0:T(1024)} dynamic-update-slice(f32[2069760]{0:T(1024)} %constant_dynamic-update-slice_fusion.5, f32[589824]{0:T(1024)S(1)} %copy-done.15, s32[]{} %constant.208) | dynamic-update-slice | bytes 4718596
  651.0 159.5 %all-reduce.5.cloned.1.call-done = f32[2069760]{0:T(1024)} async-done(((f32[2069760]{0:T(1024)}), f32[2069760]{0:T(1024)}) %all-reduce.5.cloned.1.call-update) | async-done | bytes 8279056 | tf_op jit(solution)/shard_map/psum | solution.py:229
  (319 shorter events, 292.7 us)
Async XLA Ops:
  7.2 48.1 %all-gather.5.cloned.1.call-start = ((), (), s32[]{:S(2)}) async-start(), calls=%async_computation.3 | async-start | bytes 4515840 | tf_op jit(solution)/shard_map/all_gather | solution.py:78
  21.5 67.2 %all-gather.3.cloned.1.call-start = ((), (), s32[]{:S(2)}) async-start(), calls=%async_computation.2 | async-start | bytes 4515840 | tf_op jit(solution)/shard_map/all_gather | solution.py:79
  24.8 412.9 %reduce-scatter.5.cloned.1.call-start = ((), (), s32[]{:S(2)}) async-start(), calls=%async_computation.5 | async-start | bytes 9031680 | tf_op jit(solution)/shard_map/reduce_scatter | solution.py:175
  95.0 81.8 %copy-start.7 = (f32[3,392,384]{2,1,0:T(8,128)S(1)}, f32[3,392,384]{2,1,0:T(8,128)}, u32[]{:S(2)}) copy-start(f32[3,392,384]{2,1,0:T(8,128)} %copy-done.6) | copy-start | bytes 5419012
  95.0 81.8 %copy-start.25 = (bf16[384,384]{1,0:T(8,128)(2,1)S(1)}, bf16[384,384]{1,0:T(8,128)(2,1)}, u32[]{:S(2)}) copy-start(bf16[384,384]{1,0:T(8,128)(2,1)} %param.33) | copy-start | bytes 884740
  95.0 81.8 %copy-start.60 = (f32[384]{0:T(512)S(1)}, f32[384]{0:T(512)}, u32[]{:S(2)}) copy-start(f32[384]{0:T(512)} %param.34) | copy-start | bytes 4612
  179.2 29.9 %copy-start.9 = (f32[3,392,384]{2,1,0:T(8,128)}, f32[3,392,384]{2,1,0:T(8,128)S(1)}, u32[]{:S(2)}) copy-start(f32[3,392,384]{2,1,0:T(8,128)S(1)} %get-tuple-element.220) | copy-start | bytes 5419012
  179.2 29.9 %copy-start.32 = (f32[3,392]{1,0:T(4,128)}, f32[3,392]{1,0:T(4,128)S(1)}, u32[]{:S(2)}) copy-start(f32[3,392]{1,0:T(4,128)S(1)} %broadcast_multiply_fusion) | copy-start | bytes 14116
  179.8 29.3 %copy-start.36 = (f32[3,392]{1,0:T(4,128)}, f32[3,392]{1,0:T(4,128)S(1)}, u32[]{:S(2)}) copy-start(f32[3,392]{1,0:T(4,128)S(1)} %fusion.51) | copy-start | bytes 14116
  183.6 17.4 %copy-start.18 = (bf16[3,392,384]{2,1,0:T(8,128)(2,1)S(1)}, bf16[3,392,384]{2,1,0:T(8,128)(2,1)}, u32[]{:S(2)}) copy-start(bf16[3,392,384]{2,1,0:T(8,128)(2,1)} %param.41) | copy-start | bytes 2709508
  183.6 17.4 %copy-start.30 = (bf16[1536,384]{1,0:T(8,128)(2,1)S(1)}, bf16[1536,384]{1,0:T(8,128)(2,1)}, u32[]{:S(2)}) copy-start(bf16[1536,384]{1,0:T(8,128)(2,1)} %param.39) | copy-start | bytes 3538948
  231.0 14.8 %copy-start.2 = (f32[6,392,1568]{2,1,0:T(8,128)S(1)}, f32[6,392,1568]{2,1,0:T(8,128)}, u32[]{:S(2)}) copy-start(f32[6,392,1568]{2,1,0:T(8,128)} %copy-done.1) | copy-start | bytes 44255236 | tf_op jit(solution)/shard_map/while
  337.1 14.8 %copy-start.2 = (f32[6,392,1568]{2,1,0:T(8,128)S(1)}, f32[6,392,1568]{2,1,0:T(8,128)}, u32[]{:S(2)}) copy-start(f32[6,392,1568]{2,1,0:T(8,128)} %copy-done.1) | copy-start | bytes 44255236 | tf_op jit(solution)/shard_map/while
  373.3 131.8 %reduce-scatter.3.cloned.1.call-start = ((), (), s32[]{:S(2)}) async-start(), calls=%async_computation.4 | async-start | bytes 9031680 | tf_op jit(solution)/shard_map/reduce_scatter | solution.py:174
  373.9 172.8 %all-reduce.3.cloned.1.call-start = ((), (), s32[]{:S(2)}) async-start(), calls=%async_computation.6 | async-start | bytes 737280 | tf_op jit(solution)/shard_map/psum | solution.py:194
  396.2 110.5 %copy-start.8 = (f32[3,392,384]{2,1,0:T(8,128)S(1)}, f32[3,392,384]{2,1,0:T(8,128)}, u32[]{:S(2)}) copy-start(f32[3,392,384]{2,1,0:T(8,128)} %copy-done.6) | copy-start | bytes 5419012
  396.3 110.5 %copy-start.35 = (f32[3,392]{1,0:T(4,128)S(1)}, f32[3,392]{1,0:T(4,128)}, u32[]{:S(2)}) copy-start(f32[3,392]{1,0:T(4,128)} %copy-done.34) | copy-start | bytes 14116
  396.3 110.5 %copy-start.54 = (f32[384]{0:T(512)S(1)}, f32[384]{0:T(512)}, u32[]{:S(2)}) copy-start(f32[384]{0:T(512)} %param.28) | copy-start | bytes 4612
  515.5 295.0 %all-reduce.5.cloned.1.call-start = ((), (), s32[]{:S(2)}) async-start(), calls=%async_computation.7 | async-start | bytes 16564224 | tf_op jit(solution)/shard_map/psum | solution.py:229
  554.2 28.2 %copy-start.56 = (f32[384]{0:T(512)S(1)}, f32[384]{0:T(512)}, u32[]{:S(2)}) copy-start(f32[384]{0:T(512)} %get-tuple-element.178) | copy-start | bytes 4612
  554.2 29.5 %copy-start.64 = (f32[384]{0:T(512)S(1)}, f32[384]{0:T(512)}, u32[]{:S(2)}) copy-start(f32[384]{0:T(512)} %get-tuple-element.143) | copy-start | bytes 4612
  554.2 30.8 %copy-start.63 = (f32[384]{0:T(512)S(1)}, f32[384]{0:T(512)}, u32[]{:S(2)}) copy-start(f32[384]{0:T(512)} %get-tuple-element.145) | copy-start | bytes 4612
  577.5 30.1 %copy-start.57 = (f32[1536]{0:T(1024)S(1)}, f32[1536]{0:T(1024)}, u32[]{:S(2)}) copy-start(f32[1536]{0:T(1024)} %get-tuple-element.224) | copy-start | bytes 18436
  577.5 31.4 %copy-start.15 = (f32[589824]{0:T(1024)S(1)}, f32[589824]{0:T(1024)}, u32[]{:S(2)}) copy-start(f32[589824]{0:T(1024)} %reshape.293) | copy-start | bytes 7077892
  (62 other events, 267.4 us)
Sparse Core Ops, SparseCore 0:
  21.6 33.6 all-gather.4
  57.4 31.1 all-gather.2
  373.4 64.2 reduce-scatter.4
  440.4 64.6 reduce-scatter.2
  515.6 31.0 all-reduce.2
  630.4 180.0 all-reduce.4
where the time goes:
time: 861 us; the launch traced here: 848 us
  waiting for transfers between devices  343 us (40%)
  local copies, waits for them, and re-layouts  193 us (22%)
  matrix products  181 us (21%)
  other arithmetic  106 us (12%)
  between operations  23.5 us (3%)
    psum x1, waiting for transfers between devices, shards(): summed = lax.psum(flat, ('seq', 'clip'))  159 us
    unnamed x132, local copies, waits for them, and re-layouts  79.6 us
    reduce_scatter x1, waiting for transfers between devices, shards(): lax.psum_scatter(grad_key_part, 'seq', scatter_dimension=1, tiled=True)  64.7 us
    dot_general x3, matrix products, attend_back(): jnp.einsum('qhe,khe->hqk', g_heads, v_heads, preferred_element_type=jnp.f...  43.3 us
    reduce_scatter x1, waiting for transfers between devices, shards(): lax.psum_scatter(grad_value_part, 'seq', scatter_dimension=1, tiled=True)  38 us
    dynamic_update_slice x15, local copies, waits for them, and re-layouts, shards(): lax.map(attend_back, (queries, keys_all, values_all, grad_attended, log_t...  36.6 us
    all_gather x1, waiting for transfers between devices, shards(): lax.all_gather(keys_local, 'seq', axis=1, tiled=True)  28.6 us
    all_gather x1, waiting for transfers between devices, shards(): lax.all_gather(values_local, 'seq', axis=1, tiled=True)  27 us
  transfers between devices with their start and end apart: 6, of which 6 were waited for; matrix products, arithmetic and copies ran while one was open for 7% of the time, Pallas kernels for 0%

commit v1 on v0

v1 whole, which is shorter than its diff:
```python
import functools

import jax
import jax.numpy as jnp
import numpy as np
from jax import lax
from jax.experimental import pallas as pl
from jax.experimental.pallas import tpu as pltpu
from jax.sharding import PartitionSpec as P

D = 384
HEADS = 6
HEAD = 64
PAIRS = 3
PAIR = 128
FF = 1536
DIN = 768
LEN = 1568
FC_ROWS = 3584
QKV_ROWS = 2048
STEP = 112
AXES = ("seq", "clip")
VMEM = 60 * 1024 * 1024

bf16 = jnp.bfloat16
f32 = jnp.float32


def dot(left, right):
    return lax.dot_general(
        left, right, (((1,), (0,)), ((), ())), preferred_element_type=f32
    )


def dot_rt(left, right):
    return lax.dot_general(
        left, right, (((1,), (1,)), ((), ())), preferred_element_type=f32
    )


def dot_lt(left, right):
    return lax.dot_general(
        left, right, (((0,), (0,)), ((), ())), preferred_element_type=f32
    )


def split3(value):
    high = value.astype(bf16)
    rest = value - high.astype(f32)
    middle = rest.astype(bf16)
    low = (rest - middle.astype(f32)).astype(bf16)
    return high, middle, low


def sinusoid_table(length, columns):
    positions = np.arange(length, dtype=np.float64)[:, None]
    column = np.arange(columns)
    angles = positions / np.power(10000.0, (2 * (column // 2)) / columns)[None, :]
    return np.where((column % 2)[None, :] == 0, np.sin(angles), np.cos(angles)).astype(np.float32)


def forward_kernel(
    start_ref,
    x_ref,
    pos_ref,
    table_ref,
    w_proj_ref,
    b_proj_ref,
    mask_ref,
    gain1_ref,
    bias1_ref,
    w_qkv_ref,
    q_bias_ref,
    v_bias_ref,
    w_out_ref,
    b_out_ref,
    gain2_ref,
    bias2_ref,
    w_fc1_ref,
    b_fc1_ref,
    w_fc2_ref,
    b_fc2_ref,
    cot_ref,
    out_ref,
    p_ref,
    q_ref,
    k_ref,
    v_ref,
    normed_ref,
    xhat_ref,
    rstd_ref,
    gs_ref,
    extra_ref,
    gmid_ref,
    flat_ref,
    emb_s,
    att_s,
    linv_s,
    *,
    rows,
):
    clip = pl.program_id(0)
    phase = pl.program_id(1)
    lane = lax.broadcasted_iota(jnp.int32, (1, PAIR), 1)

    @pl.when(jnp.logical_and(clip == 0, phase == 0))
    def _():
        flat_ref[...] = jnp.zeros_like(flat_ref)

    @pl.when(phase == 0)
    def _():
        projected = dot(x_ref[0], w_proj_ref[...]) + b_proj_ref[...][None, :]
        high, middle, low = split3(projected - mask_ref[...][None, :])
        row = lax.broadcasted_iota(jnp.int32, (LEN, 1), 0)
        onehot = (row == pos_ref[0]).astype(f32).astype(bf16)
        emb_s[...] = (
            (table_ref[...].reshape(LEN, D) + mask_ref[...][None, :]) + dot(onehot, low) + dot(onehot, middle)
        ) + dot(onehot, high)

        def norm_rows(step, carry):
            at = pl.ds(pl.multiple_of(step * STEP, STEP), STEP)
            value = emb_s[at, :]
            centered = value - jnp.mean(value, axis=1, keepdims=True)
            rstd = lax.rsqrt(jnp.mean(centered * centered, axis=1, keepdims=True) + 1e-05)
            xhat = centered * rstd
            xhat_ref[0, at, :] = xhat.astype(bf16)
            normed_ref[0, at, :] = (xhat * gain1_ref[...][None, :] + bias1_ref[...][None, :]).astype(bf16)
            rstd_ref[0, at, :] = rstd
            return carry

        lax.fori_loop(0, LEN // STEP, norm_rows, 0)
        normed = normed_ref[0]
        k_ref[0] = dot(normed, w_qkv_ref[:, D : 2 * D]).astype(bf16)
        v_ref[0] = (dot(normed, w_qkv_ref[:, 2 * D :]) + v_bias_ref[...][None, :]).astype(bf16)
        q_ref[0] = (dot(normed[:rows], w_qkv_ref[:, :D]) + q_bias_ref[...][None, :]).astype(bf16)

    @pl.when(jnp.logical_and(phase >= 1, phase <= PAIRS))
    def _():
        at = pl.ds(pl.multiple_of((phase - 1) * PAIR, PAIR), PAIR)
        query = q_ref[0, :, at]
        key = k_ref[0, :, at]
        value = jnp.concatenate([v_ref[0, :, at], jnp.ones((LEN, PAIR), bf16)], axis=1)
        parts = []
        for head in range(2):
            own = (lane < HEAD) if head == 0 else (lane >= HEAD)
            scores = dot_rt(jnp.where(own, query, jnp.zeros_like(query)), key)
            largest = jnp.max(scores, axis=1, keepdims=True)
            weights = jnp.exp2((scores - largest) * (HEAD**-0.5 * np.log2(np.e))).astype(bf16)
            p_ref[0, head] = weights
            parts.append(dot(weights, value))
        sums = jnp.where(lane < HEAD, parts[0][:, PAIR:], parts[1][:, PAIR:])
        inverse = 1.0 / sums
        linv_s[:, at] = inverse
        att_s[:, at] = jnp.where(lane < HEAD, parts[0][:, :PAIR], parts[1][:, :PAIR]) * inverse

    @pl.when(phase == PAIRS + 1)
    def _():
        att = att_s[...]
        attended = att.astype(bf16)
        middle = emb_s[:rows, :] + (dot(attended, w_out_ref[...]) + b_out_ref[...][None, :])
        centered = middle - jnp.mean(middle, axis=1, keepdims=True)
        rstd = lax.rsqrt(jnp.mean(centered * centered, axis=1, keepdims=True) + 1e-05)
        xhat = centered * rstd
        normed2 = (xhat * gain2_ref[...][None, :] + bias2_ref[...][None, :]).astype(bf16)
        cot = cot_ref[0]
        cot_f = cot.astype(f32)
        output = middle + b_fc2_ref[...][None, :]
        grad_normed = jnp.zeros((rows, D), f32)
        width = 256
        for block in range(FF // width):
            at = slice(block * width, (block + 1) * width)
            pre = dot(normed2, w_fc1_ref[:, at]) + b_fc1_ref[at][None, :]
            cdf = 0.5 + 0.5 * lax.erf(pre * np.float32(0.5**0.5))
            hidden = (pre * cdf).astype(bf16)
            output = output + dot(hidden, w_fc2_ref[at, :])
            flat_ref[at, :] += dot_lt(hidden, cot)
            slope = cdf + pre * (jnp.exp2(pre * pre * (-0.5 * np.log2(np.e))) * ((2 * np.pi) ** -0.5))
            grad_pre = dot_rt(cot, w_fc2_ref[at, :]) * slope
            grad_pre_b = grad_pre.astype(bf16)
            col_sum = jnp.sum(grad_pre_b.astype(f32), axis=0, keepdims=True)
            grad_w = dot_lt(normed2, grad_pre_b)
            for piece in range(width // PAIR):
                col = block * width + piece * PAIR
                first = FF + D + (col // D) * D
                lanes = slice(col % D, col % D + PAIR)
                src = slice(piece * PAIR, (piece + 1) * PAIR)
                flat_ref[first : first + D, lanes] += grad_w[:, src]
                vec_row = 2 * FF + D + col // D
                flat_ref[vec_row : vec_row + 1, lanes] += col_sum[:, src]
            grad_normed = grad_normed + dot_rt(grad_pre_b, w_fc1_ref[:, at])
        out_ref[0] = output.astype(bf16)
        base = 2 * FF + D + 4
        flat_ref[base : base + 1, :] += jnp.sum(cot_f, axis=0, keepdims=True)
        flat_ref[base + 1 : base + 2, :] += jnp.sum(grad_normed * xhat, axis=0, keepdims=True)
        flat_ref[base + 2 : base + 3, :] += jnp.sum(grad_normed, axis=0, keepdims=True)
        scaled = grad_normed * gain2_ref[...][None, :]
        grad_middle = cot_f + rstd * (
            scaled
            - jnp.mean(scaled, axis=1, keepdims=True)
            - xhat * jnp.mean(scaled * xhat, axis=1, keepdims=True)
        )
        gmid_ref[0] = grad_middle
        grad_branch = grad_middle.astype(bf16)
        flat_ref[base + 3 : base + 4, :] += jnp.sum(
            grad_branch.astype(f32), axis=0, keepdims=True
        )
        flat_ref[FF : FF + D, :] += dot_lt(attended, grad_branch)
        grad_att = dot_rt(grad_branch, w_out_ref[...]).astype(bf16).astype(f32)
        grad_s = (grad_att * linv_s[...]).astype(bf16)
        gs_ref[0] = grad_s
        product = grad_s.astype(f32) * att
        for pair in range(PAIRS):
            piece = product[:, pair * PAIR : (pair + 1) * PAIR]
            for head in range(2):
                own = (lane < HEAD) if head == 0 else (lane >= HEAD)
                inner = -jnp.sum(jnp.where(own, piece, 0.0), axis=1, keepdims=True)
                high, middle3, low = split3(inner)
                filled = jnp.where(
                    lane == 0,
                    high.astype(f32),
                    jnp.where(
                        lane == 1,
                        middle3.astype(f32),
                        jnp.where(lane == 2, low.astype(f32), 0.0),
                    ),
                )
                first = (2 * pair + head) * PAIR
                extra_ref[0, :, first : first + PAIR] = filled.astype(bf16)


def backward_kernel(
    start_ref,
    q_ref,
    k_ref,
    v_ref,
    gs_ref,
    extra_ref,
    p_ref,
    normed_ref,
    xhat_ref,
    rstd_ref,
    gmid_ref,
    x_ref,
    pos_ref,
    w_qkv_ref,
    gain1_ref,
    flat_ref,
    gproj_ref,
    dq_s,
    dk_s,
    dv_s,
    gn_s,
    own_s,
    high_s,
    low_s,
    *,
    rows,
):
    clip = pl.program_id(0)
    phase = pl.program_id(1)
    lane = lax.broadcasted_iota(jnp.int32, (1, PAIR), 1)

    @pl.when(jnp.logical_and(clip == 0, phase == 0))
    def _():
        flat_ref[...] = jnp.zeros_like(flat_ref)

    @pl.when(phase < PAIRS)
    def _():
        at = pl.ds(pl.multiple_of(phase * PAIR, PAIR), PAIR)
        query = q_ref[0, :, at] * jnp.asarray(HEAD**-0.5, bf16)
        key = k_ref[0, :, at]
        value = jnp.concatenate([v_ref[0, :, at], jnp.ones((LEN, PAIR), bf16)], axis=1)
        grad = gs_ref[0, :, at]
        queries, keys, values = [], [], []
        for head in range(2):
            own = (lane < HEAD) if head == 0 else (lane >= HEAD)
            where = pl.ds(pl.multiple_of(phase * (2 * PAIR) + head * PAIR, PAIR), PAIR)
            left = jnp.concatenate(
                [jnp.where(own, grad, jnp.zeros_like(grad)), extra_ref[0, :, where]], axis=1
            )
            weights = p_ref[0, head]
            grad_scores = (weights.astype(f32) * dot_rt(left, value)).astype(bf16)
            queries.append(dot(grad_scores, key))
            keys.append(dot_lt(grad_scores, query))
            values.append(dot_lt(weights, grad))
        dq_s[:, at] = (
            jnp.where(lane < HEAD, queries[0], queries[1]) * (HEAD**-0.5)
        ).astype(bf16)
        dk_s[:, at] = jnp.where(lane < HEAD, keys[0], keys[1]).astype(bf16)
        dv_s[:, at] = jnp.where(lane < HEAD, values[0], values[1]).astype(bf16)

    @pl.when(phase == PAIRS)
    def _():
        normed = normed_ref[0]
        grad_q = dq_s[...]
        grad_k = dk_s[...]
        grad_v = dv_s[...]
        flat_ref[:D, :] += dot_lt(normed[:rows], grad_q)
        flat_ref[D : 2 * D, :] += dot_lt(normed, grad_k)
        flat_ref[2 * D : 3 * D, :] += dot_lt(normed, grad_v)
        base = 3 * D + DIN
        ones = jnp.ones((8, LEN), bf16)
        flat_ref[base + 4 : base + 5, :] += dot(ones[:, :rows], grad_q)[:1]
        flat_ref[base + 5 : base + 6, :] += dot(ones, grad_v)[:1]
        gn_s[...] = dot_rt(grad_k, w_qkv_ref[:, D : 2 * D]) + dot_rt(
            grad_v, w_qkv_ref[:, 2 * D :]
        )
        gn_s[:rows, :] += dot_rt(grad_q, w_qkv_ref[:, :D])
        own_s[:rows, :] = gmid_ref[0]
        own_s[rows:, :] = jnp.zeros_like(own_s[rows:, :])

        def norm_rows(step, carry, with_own):
            at = pl.ds(pl.multiple_of(step * STEP, STEP), STEP)
            sum_gain, sum_bias, sum_emb = carry
            value = gn_s[at, :]
            xhat = xhat_ref[0, at, :].astype(f32)
            sum_bias = sum_bias + jnp.sum(value, axis=0, keepdims=True)
            sum_gain = sum_gain + jnp.sum(value * xhat, axis=0, keepdims=True)
            scaled = value * gain1_ref[...][None, :]
            grad = rstd_ref[0, at, :] * (
                scaled
                - jnp.mean(scaled, axis=1, keepdims=True)
                - xhat * jnp.mean(scaled * xhat, axis=1, keepdims=True)
            )
            if with_own:
                grad = grad + own_s[at, :]
            sum_emb = sum_emb + jnp.sum(grad, axis=0, keepdims=True)
            high = grad.astype(bf16)
            high_s[at, :] = high
            low_s[at, :] = (grad - high.astype(f32)).astype(bf16)
            return sum_gain, sum_bias, sum_emb

        zero = jnp.zeros((1, D), f32)
        own_steps = own_s.shape[0] // STEP
        carry = lax.fori_loop(
            0, own_steps, functools.partial(norm_rows, with_own=True), (zero, zero, zero)
        )
        sum_gain, sum_bias, sum_emb = lax.fori_loop(
            own_steps, LEN // STEP, functools.partial(norm_rows, with_own=False), carry
        )
        column = lax.broadcasted_iota(jnp.int32, (1, LEN), 1)
        onehot = (pos_ref[0] == column).astype(f32).astype(bf16)
        grad_proj = dot(onehot, high_s[...]) + dot(onehot, low_s[...])
        gproj_ref[0] = grad_proj
        sum_proj = jnp.sum(grad_proj, axis=0, keepdims=True)
        flat_ref[base : base + 1, :] += sum_proj
        flat_ref[base + 1 : base + 2, :] += sum_emb - sum_proj
        flat_ref[base + 2 : base + 3, :] += sum_gain
        flat_ref[base + 3 : base + 4, :] += sum_bias
        flat_ref[3 * D : 3 * D + DIN, :] += dot_lt(x_ref[0], grad_proj.astype(bf16))


def whole(shape):
    return pl.BlockSpec(
        shape, lambda c, h, s: (0,) * len(shape), pipeline_mode=pl.Buffered(1)
    )


def per_clip(*shape):
    return pl.BlockSpec((1,) + shape, lambda c, h, s: (c,) + (0,) * len(shape))


def run_forward(start, x_vis, local_pos, table, params, cotangent, rows):
    clips, visible, _ = x_vis.shape
    (
        w_proj,
        b_proj,
        mask_token,
        ln1_gain,
        ln1_bias,
        w_qkv,
        q_bias,
        v_bias,
        w_out,
        b_out,
        ln2_gain,
        ln2_bias,
        w_fc1,
        b_fc1,
        w_fc2,
        b_fc2,
    ) = params
    arrays = [
        (w_proj, (DIN, D)),
        (b_proj, (D,)),
        (mask_token, (D,)),
        (ln1_gain, (D,)),
        (ln1_bias, (D,)),
        (w_qkv, (D, 3 * D)),
        (q_bias, (D,)),
        (v_bias, (D,)),
        (w_out, (D, D)),
        (b_out, (D,)),
        (ln2_gain, (D,)),
        (ln2_bias, (D,)),
        (w_fc1, (D, FF)),
        (b_fc1, (FF,)),
        (w_fc2, (FF, D)),
        (b_fc2, (D,)),
    ]
    shape = jax.ShapeDtypeStruct
    return pl.pallas_call(
        functools.partial(forward_kernel, rows=rows),
        grid_spec=pltpu.PrefetchScalarGridSpec(
            num_scalar_prefetch=1,
            grid=(clips, PAIRS + 2),
            in_specs=[
                per_clip(visible, DIN),
                per_clip(1, visible),
                pl.BlockSpec(
                    (pl.Element(LEN // 8), pl.Element(8), pl.Element(D)),
                    lambda c, h, s: (s[0], 0, 0),
                ),
            ]
            + [whole(size) for _, size in arrays]
            + [per_clip(rows, D)],
            out_specs=[
                per_clip(rows, D),
                pl.BlockSpec(
                    (1, 2, rows, LEN),
                    lambda c, h, s: (c, jnp.clip(h - 1, 0, PAIRS - 1), 0, 0),
                ),
                per_clip(rows, D),
                per_clip(LEN, D),
                per_clip(LEN, D),
                per_clip(LEN, D),
                per_clip(LEN, D),
                per_clip(LEN, 1),
                per_clip(rows, D),
                per_clip(rows, HEADS * PAIR),
                per_clip(rows, D),
                whole((FC_ROWS, D)),
            ],
            scratch_shapes=[
                pltpu.VMEM((LEN, D), f32),
                pltpu.VMEM((rows, D), f32),
                pltpu.VMEM((rows, D), f32),
            ],
        ),
        out_shape=[
            shape((clips, rows, D), bf16),
            shape((clips, HEADS, rows, LEN), bf16),
            shape((clips, rows, D), bf16),
            shape((clips, LEN, D), bf16),
            shape((clips, LEN, D), bf16),
            shape((clips, LEN, D), bf16),
            shape((clips, LEN, D), bf16),
            shape((clips, LEN, 1), f32),
            shape((clips, rows, D), bf16),
            shape((clips, rows, HEADS * PAIR), bf16),
            shape((clips, rows, D), f32),
            shape((FC_ROWS, D), f32),
        ],
        compiler_params=pltpu.CompilerParams(
            dimension_semantics=("arbitrary", "arbitrary"), vmem_limit_bytes=VMEM
        ),
        name="forward_clip",
    )(
        start,
        x_vis,
        local_pos[:, None, :],
        table,
        *[value for value, _ in arrays],
        cotangent,
    )


def run_backward(start, saved, x_vis, local_pos, w_qkv, ln1_gain, rows):
    clips, visible, _ = x_vis.shape
    query, key, value, grads, extra, weights, normed, xhat, rstd, gmid = saved
    own_rows = -(-rows // STEP) * STEP
    shape = jax.ShapeDtypeStruct
    return pl.pallas_call(
        functools.partial(backward_kernel, rows=rows),
        grid_spec=pltpu.PrefetchScalarGridSpec(
            num_scalar_prefetch=1,
            grid=(clips, PAIRS + 1),
            in_specs=[
                per_clip(rows, D),
                per_clip(LEN, D),
                per_clip(LEN, D),
                per_clip(rows, D),
                per_clip(rows, HEADS * PAIR),
                pl.BlockSpec(
                    (1, 2, rows, LEN),
                    lambda c, h, s: (c, jnp.minimum(h, PAIRS - 1), 0, 0),
                ),
                per_clip(LEN, D),
                per_clip(LEN, D),
                per_clip(LEN, 1),
                per_clip(rows, D),
                per_clip(visible, DIN),
                per_clip(visible, 1),
                whole((D, 3 * D)),
                whole((D,)),
            ],
            out_specs=[whole((QKV_ROWS, D)), per_clip(visible, D)],
            scratch_shapes=[
                pltpu.VMEM((rows, D), bf16),
                pltpu.VMEM((LEN, D), bf16),
                pltpu.VMEM((LEN, D), bf16),
                pltpu.VMEM((LEN, D), f32),
                pltpu.VMEM((own_rows, D), f32),
                pltpu.VMEM((LEN, D), bf16),
                pltpu.VMEM((LEN, D), bf16),
            ],
        ),
        out_shape=[shape((QKV_ROWS, D), f32), shape((clips, visible, D), f32)],
        compiler_params=pltpu.CompilerParams(
            dimension_semantics=("arbitrary", "arbitrary"), vmem_limit_bytes=VMEM
        ),
        name="backward_clip",
    )(
        start,
        query,
        key,
        value,
        grads,
        extra,
        weights,
        normed,
        xhat,
        rstd,
        gmid,
        x_vis,
        local_pos[:, :, None],
        w_qkv,
        ln1_gain,
    )


def exchange_stages(seq_size, clip_size):
    def seq_bit(s, c):
        return (s >> 1) & 1

    def clip_bit(s, c):
        return c & 1

    def core(s, c):
        return s & 1

    stages = [(core, lambda s, c: (s ^ 1, c))]
    stages.append(
        (
            lambda s, c: seq_bit(s, c) * (1 - core(s, c)) + clip_bit(s, c) * core(s, c),
            lambda s, c: (s ^ 2, c) if s & 1 == 0 else (s, c ^ 1),
        )
    )
    stages.append(
        (
            lambda s, c: clip_bit(s, c) * (1 - core(s, c)) + seq_bit(s, c) * core(s, c),
            lambda s, c: (s, c ^ 1) if s & 1 == 0 else (s ^ 2, c),
        )
    )
    for bit in range(1, clip_size.bit_length() - 1):
        stages.append(
            (
                lambda s, c, bit=bit: (c >> bit) & 1,
                lambda s, c, bit=bit: (s, c ^ (1 << bit)),
            )
        )
    result = []
    for bit_of, partner in stages:
        pairs = []
        for s in range(seq_size):
            for c in range(clip_size):
                other = partner(s, c)
                pairs.append((s * clip_size + c, other[0] * clip_size + other[1]))
        result.append((bit_of, pairs))
    return result


def sum_everywhere(flat):
    seq_size = lax.axis_size("seq")
    clip_size = lax.axis_size("clip")
    s = lax.axis_index("seq")
    c = lax.axis_index("clip")
    stages = exchange_stages(seq_size, clip_size)
    data = flat
    for bit_of, pairs in stages:
        half = data.shape[0] // 2
        bit = bit_of(s, c)
        sent = lax.dynamic_slice_in_dim(data, (1 - bit) * half, half, 0).astype(bf16)
        kept = lax.dynamic_slice_in_dim(data, bit * half, half, 0)
        data = kept + lax.ppermute(sent, AXES, pairs).astype(f32)
    data = data.astype(bf16)
    for bit_of, pairs in stages[::-1]:
        bit = bit_of(s, c)
        other = lax.ppermute(data, AXES, pairs)
        data = jnp.where(
            bit == 0, jnp.concatenate([data, other]), jnp.concatenate([other, data])
        )
    return data.astype(f32)


def sum_over_seq(value):
    s = lax.axis_index("seq")
    core_pairs = [(0, 1), (1, 0), (2, 3), (3, 2)]
    chip_pairs = [(0, 2), (2, 0), (1, 3), (3, 1)]
    half = value.shape[0] // 2
    bit = s & 1
    sent = lax.dynamic_slice_in_dim(value, (1 - bit) * half, half, 0).astype(bf16)
    kept = lax.dynamic_slice_in_dim(value, bit * half, half, 0)
    part = (kept + lax.ppermute(sent, "seq", core_pairs).astype(f32)).astype(bf16)
    other = lax.ppermute(part, "seq", chip_pairs)
    part = (part.astype(f32) + other.astype(f32)).astype(bf16)
    other = lax.ppermute(part, "seq", core_pairs)
    return jnp.where(bit == 0, jnp.concatenate([part, other]), jnp.concatenate([other, part]))


def shards(x_vis, vis_pos, *rest):
    params, cotangent = rest[:-1], rest[-1]
    w_proj, ln1_gain, w_qkv = params[0], params[3], params[5]
    rows = LEN // lax.axis_size("seq")
    clips, visible, _ = x_vis.shape
    first = lax.axis_index("seq") * rows
    local_pos = jnp.where(vis_pos >= first, vis_pos - first, vis_pos - first + LEN)
    table = sinusoid_table(LEN, D)
    table = jnp.asarray(np.concatenate([table, table[: LEN - rows]]).reshape(-1, 8, D))
    start = jnp.reshape(first // 8, (1,)).astype(jnp.int32)
    output, weights, query, key, value, normed, xhat, rstd, grads, extra, gmid, flat_fc = (
        run_forward(start, x_vis, local_pos, table, params, cotangent, rows)
    )
    saved = (query, key, value, grads, extra, weights, normed, xhat, rstd, gmid)
    flat_qkv, grad_proj = run_backward(start, saved, x_vis, local_pos, w_qkv, ln1_gain, rows)

    fc = sum_everywhere(flat_fc)
    qkv = sum_everywhere(flat_qkv)
    count = clips * visible
    padded = -(-count // 32) * 32
    stacked = jnp.pad(grad_proj.reshape(count, D), ((0, padded - count), (0, 0)))
    grad_projected = sum_over_seq(stacked)[:count]
    grad_x = lax.dot_general(
        grad_projected, w_proj, (((1,), (1,)), ((), ())), preferred_element_type=f32
    ).reshape(clips, visible, DIN)

    grad_w_qkv = jnp.concatenate([qkv[:D], qkv[D : 2 * D], qkv[2 * D : 3 * D]], axis=1)
    grad_w_proj = qkv[3 * D : 3 * D + DIN]
    base = 3 * D + DIN
    grad_b_proj, grad_mask, grad_ln1_gain, grad_ln1_bias, grad_q_bias, grad_v_bias = [
        qkv[base + number] for number in range(6)
    ]
    grad_w_fc2 = fc[:FF]
    grad_w_out = fc[FF : FF + D]
    grad_w_fc1 = jnp.concatenate(
        [fc[FF + D + number * D : FF + 2 * D + number * D] for number in range(4)], axis=1
    )
    base = 2 * FF + D
    grad_b_fc1 = fc[base : base + 4].reshape(FF)
    grad_b_fc2, grad_ln2_gain, grad_ln2_bias, grad_b_out = [
        fc[base + 4 + number] for number in range(4)
    ]

    def ratio(weight, grad):
        return jnp.sqrt(jnp.mean(weight.astype(f32) ** 2)) / jnp.sqrt(jnp.mean(grad**2) + 1e-06)

    trust = jnp.stack(
        [
            ratio(w_proj, grad_w_proj),
            ratio(params[8], grad_w_out),
            ratio(params[12], grad_w_fc1),
            ratio(params[14], grad_w_fc2),
        ]
    )
    trust_qkv = ratio(w_qkv, grad_w_qkv).reshape(1)
    return (
        output,
        grad_x,
        grad_w_proj,
        grad_b_proj,
        grad_mask,
        grad_ln1_gain,
        grad_ln1_bias,
        grad_w_qkv,
        grad_q_bias,
        grad_v_bias,
        grad_w_out,
        grad_b_out,
        grad_ln2_gain,
        grad_ln2_bias,
        grad_w_fc1,
        grad_b_fc1,
        grad_w_fc2,
        grad_b_fc2,
        trust,
        trust_qkv,
    )


def solution(mesh):
    return jax.shard_map(
        shards,
        mesh=mesh,
        in_specs=(P("clip", None, None), P("clip", None))
        + (P(),) * 16
        + (P("clip", "seq", None),),
        out_specs=(P("clip", "seq", None), P("clip", None, None)) + (P(),) * 18,
        check_vma=False,
    )
```

time: 861 us -> 266 us (0.31); the launches traced: 848 us -> 265 us
  waiting for transfers between devices: 343 us -> 13.8 us
  local copies, waits for them, and re-layouts: 193 us -> 13.4 us
  matrix products: 181 us -> 1.69 us
  Pallas kernels: 0 us -> 142 us
  other arithmetic: 106 us -> 37.8 us
  starting transfers between devices: 0.92 us -> 47.2 us
  between operations: 23.5 us -> 9.02 us
    psum x2 -> x0, waiting for transfers between devices: 184 us -> none  [the longest x1 159 us: shards(): summed = lax.psum(flat, ('seq', 'clip'))]
    dot_general x38 -> x1, matrix products: 181 us -> 1.69 us  [shards(): lax.dot_general(grad_projected, w_proj, (((1,), (1,)), ((), ())), preferr...]
    pallas_call x0 -> x2, Pallas kernels: none -> 142 us  [the longest x1 78.1 us: run_forward(): pl.pallas_call(functools.partial(forward_kernel, rows=rows), grid_spec=pl...]
    reduce_scatter x2 -> x0, waiting for transfers between devices: 103 us -> none  [the longest x1 64.7 us: shards(): lax.psum_scatter(grad_key_part, 'seq', scatter_dimension=1, tiled=True)]
    unnamed x132 -> x14, local copies, waits for them, and re-layouts: 79.6 us -> 0.04 us
    all_gather x2 -> x0, waiting for transfers between devices: 55.6 us -> none  [the longest x1 28.6 us: shards(): lax.all_gather(keys_local, 'seq', axis=1, tiled=True)]
    ppermute x0 -> x23, starting transfers between devices: none -> 47.2 us  [the longest x10 28.7 us: sum_everywhere(): other = lax.ppermute(data, AXES, pairs)]
    reduce_sum x22 -> x9, other arithmetic: 57 us -> 15.6 us  [the longest x4 9.22 us: ratio(): jnp.mean(grad ** 2) + 1e-06]
  transfers between devices with their start and end apart: 6 -> 23, of which waited for: 6 -> 9; matrix products, arithmetic and copies ran while one was open for 7% -> 14% of each run, Pallas kernels for 0% -> 24%
where the time goes in v1:
time: 266 us; the launch traced here: 265 us
  Pallas kernels  142 us (53%)
  starting transfers between devices  47.2 us (18%)
  other arithmetic  37.8 us (14%)
  waiting for transfers between devices  13.8 us (5%)
  local copies, waits for them, and re-layouts  13.4 us (5%)
  between operations  9.02 us (3%)
    pallas_call x1, Pallas kernels, run_forward(): pl.pallas_call(functools.partial(forward_kernel, rows=rows), grid_spec=pl...  78.1 us
    pallas_call x1, Pallas kernels, run_backward(): pl.pallas_call(functools.partial(backward_kernel, rows=rows), grid_spec=p...  63.5 us
    ppermute x10, starting transfers between devices, sum_everywhere(): other = lax.ppermute(data, AXES, pairs)  28.7 us
    ppermute x10, starting transfers between devices, sum_everywhere(): data = kept + lax.ppermute(sent, AXES, pairs).astype(f32)  13.6 us
    ppermute x10, waiting for transfers between devices, sum_everywhere(): data = kept + lax.ppermute(sent, AXES, pairs).astype(f32)  10.2 us
    reduce_sum x4, other arithmetic, ratio(): jnp.mean(grad ** 2) + 1e-06  9.22 us
    add x8, other arithmetic, sum_everywhere(): data = kept + lax.ppermute(sent, AXES, pairs).astype(f32)  6.69 us
    reduce_sum x5, other arithmetic, ratio(): jnp.mean(weight.astype(f32) ** 2)  6.39 us
  transfers between devices with their start and end apart: 23, of which 9 were waited for; matrix products, arithmetic and copies ran while one was open for 14% of the time, Pallas kernels for 24%

profile of v1, /device:TPU:1, one launch (start us, length us, event | category | flops | bytes accessed | tf_op | source)
XLA Modules:
  0.0 264.6 jit_solution(3572925876310662227)
XLA Ops:
  1.9 78.1 %forward_clip.1 = (bf16[3,392,384]{2,1,0:T(8,128)(2,1)}, bf16[3,6,392,1568]{3,2,1,0:T(8,128)(2,1)}, bf16[3,392,384]{2,1,0:T(8,128)(2,1)}, bf16[3,1568,384]{2,1,0...) custom-call(s32[1]{0:T(128)} %bitcast.start_ref, ...), custom_call_target="tpu_custom_call" | custom-call | tf_op jit(solution)/shard_map/forward_clip/pallas_call | solution.py:402
  80.1 1.9 dynamic-slice_convert_fusion
  83.0 63.5 %backward_clip.1 = (f32[2048,384]{1,0:T(8,128)}, f32[3,157,384]{2,1,0:T(8,128)}) custom-call(s32[1]{0:T(128)} %bitcast.start_ref, bf16[3,392,384]{2,1,0:T(8,128)(2,1)} %get-tuple-element.35.q_ref, bf16[3,1568,384]{2,1,0:T(8,128)(2,1)} %get-tuple-element.36.k_ref, bf16[3,1568,384]{2,1,0:T(8,128)(2,1)} %get-tuple-element.37.v_ref, ...), custom_call_target="tpu_custom_call" | custom-call | tf_op jit(solution)/shard_map/backward_clip/pallas_call | solution.py:473
  148.6 1.9 collective-permute-done.3
  152.9 2.6 collective-permute-start.4
  155.5 2.4 convert_add_fusion
  161.5 2.5 multiply_reduce_fusion.1
  166.8 2.8 %collective-permute-done.14 = bf16[896,384]{1,0:T(8,128)(2,1)} collective-permute-done((bf16[896,384]{1,0:T(8,128)(2,1)}, bf16[896,384]{1,0:T(8,128)(2,1)}, u32[]{:S(2)}, u32[]{:S(2)}) %collective-permute-start.14) | collective-permute-done | bytes 688160 | tf_op jit(solution)/shard_map/ppermute | solution.py:585
  173.6 3.8 %collective-permute-done.15 = bf16[448,384]{1,0:T(8,128)(2,1)S(1)} collective-permute-done((bf16[448,384]{1,0:T(8,128)(2,1)S(1)}, bf16[448,384]{1,0:T(8,128)(2,1)S(1)}, u32[]{:S(2)}, u32[]{:S(2)}) %collective-permute-start.15) | collective-permute-done | bytes 344096 | tf_op jit(solution)/shard_map/ppermute | solution.py:585
  178.9 2.4 collective-permute-start.7
  181.9 2.3 collective-permute-start.17
  186.3 2.9 %collective-permute-start.18 = (bf16[112,384]{1,0:T(8,128)(2,1)S(1)}, bf16[112,384]{1,0:T(8,128)(2,1)S(1)}, u32[]{:S(2)}, u32[]{:S(2)}) collective-permute-start(bf16[112,384]{1,0:T(8,128)(2,1)S(1)} %add_convert_fusion.1), channel_id=1, source_target_pairs={{0,4},{1,5},{2,6},{3,7},{4,0},{5,1},{6,2},{7,3},{8,12},{9,13},{10,... | collective-permute-start | bytes 258056 | tf_op jit(solution)/shard_map/ppermute | solution.py:589
  189.3 3.1 %collective-permute-start.9 = (bf16[128,384]{1,0:T(8,128)(2,1)S(1)}, bf16[128,384]{1,0:T(8,128)(2,1)S(1)}, u32[]{:S(2)}, u32[]{:S(2)}) collective-permute-start(bf16[128,384]{1,0:T(8,128)(2,1)S(1)} %maximum_select_fusion.9), channel_id=1, source_target_pairs={{0,2},{1,3},{2,0},{3,1},{4,6},{5,7},{6,4},{7,5},{8,10},{9,11},{10,... | collective-permute-start | bytes 294920 | tf_op jit(solution)/shard_map/ppermute | solution.py:589
  192.4 2.9 %collective-permute-start.19 = (bf16[224,384]{1,0:T(8,128)(2,1)S(1)}, bf16[224,384]{1,0:T(8,128)(2,1)S(1)}, u32[]{:S(2)}, u32[]{:S(2)}) collective-permute-start(bf16[224,384]{1,0:T(8,128)(2,1)S(1)} %maximum_select_fusion.8), channel_id=1, source_target_pairs={{0,2},{1,3},{2,0},{3,1},{4,6},{5,7},{6,4},{7,5},{8,10},{9,11},{10,... | collective-permute-start | bytes 516104 | tf_op jit(solution)/shard_map/ppermute | solution.py:589
  211.4 13.8 %collective-permute-start.12 = (bf16[1024,384]{1,0:T(8,128)(2,1)S(1)}, bf16[1024,384]{1,0:T(8,128)(2,1)}, u32[]{:S(2)}, u32[]{:S(2)}) collective-permute-start(bf16[1024,384]{1,0:T(8,128)(2,1)S(1)} %maximum_select_fusion.3), channel_id=1, source_target_pairs={{0,8},{1,9},{2,10},{3,11},{4,12},{5,13},{6,14},{7,15},{8,0},{9,1},... | collective-permute-start | bytes 2359304 | tf_op jit(solution)/shard_map/ppermute | solution.py:589
  229.5 4.2 %collective-permute-start.2 = (bf16[240,384]{1,0:T(8,128)(2,1)S(1)}, bf16[240,384]{1,0:T(8,128)(2,1)S(1)}, u32[]{:S(2)}, u32[]{:S(2)}) collective-permute-start(bf16[240,384]{1,0:T(8,128)(2,1)S(1)} %add_convert_fusion), channel_id=1, source_target_pairs={{0,8},{8,0},{16,24},{24,16},{1,9},{9,1},{17,25},{25,17},{2,10},{10... | collective-permute-start | bytes 552968 | tf_op jit(solution)/shard_map/ppermute | solution.py:607
  233.7 2.7 %maximum_select_fusion.2 = bf16[1792,384]{1,0:T(8,128)(2,1)} fusion(bf16[896,384]{1,0:T(8,128)(2,1)} %collective-permute-done.21, bf16[896,384]{1,0:T(8,128)(2,1)S(1)} %maximum_select_fusion.4, pred[]{:T(512)S(6)} %eq.22), kind=kLoop, calls=%fused_computation.16 | loop fusion | flops 6193152 | bytes 2752513 | tf_op jit(solution)/shard_map/jit(_where)/select_n | solution.py:590
  238.1 2.6 reshape.57
  240.7 2.4 fusion.1
  243.1 1.8 multiply_reduce_fusion.6
  245.8 2.2 multiply_reduce_fusion.4
  249.3 3.4 %fusion = f32[3584,384]{1,0:T(8,128)S(1)} fusion(bf16[1792,384]{1,0:T(8,128)(2,1)} %collective-permute-done.22, bf16[1792,384]{1,0:T(8,128)(2,1)} %maximum_select_fusion.2, pred[]{:T(512)S(6)} %eq.10), kind=kLoop, calls=%fused_computation.1 | loop fusion | flops 13762560 | bytes 8257537 | tf_op jit(solution)/shard_map/convert_element_type | solution.py:593
  254.9 2.5 multiply_reduce_fusion
  258.8 2.6 multiply_reduce_fusion.2
  (94 shorter events, 44.0 us)
Async XLA Ops:
  82.0 73.5 %collective-permute-start.13 = (bf16[1792,384]{1,0:T(8,128)(2,1)S(1)}, bf16[1792,384]{1,0:T(8,128)(2,1)}, u32[]{:S(2)}, u32[]{:S(2)}) collective-permute-start(bf16[1792,384]{1,0:T(8,128)(2,1)S(1)} %dynamic-slice_convert_fusion), channel_id=1, source_target_pairs={{0,8},{1,9},{2,10},{3,11},{4,12},{5,13},{6,14},{7,15},{8,0},{9,1},... | collective-permute-start | bytes 4128776 | tf_op jit(solution)/shard_map/ppermute | solution.py:585
  148.0 2.4 collective-permute-start.3
  152.9 11.1 %collective-permute-start.4 = (bf16[512,384]{1,0:T(8,128)(2,1)}, bf16[512,384]{1,0:T(8,128)(2,1)}, u32[]{:S(2)}, u32[]{:S(2)}) collective-permute-start(bf16[512,384]{1,0:T(8,128)(2,1)} %dynamic-slice_convert_fusion.3), channel_id=1, source_target_pairs={{0,16},{1,17},{2,18},{3,19},{4,20},{5,21},{6,22},{7,23},{8,9},{9,8... | collective-permute-start | bytes 1179656 | tf_op jit(solution)/shard_map/ppermute | solution.py:585
  158.9 10.7 %collective-permute-start.14 = (bf16[896,384]{1,0:T(8,128)(2,1)}, bf16[896,384]{1,0:T(8,128)(2,1)}, u32[]{:S(2)}, u32[]{:S(2)}) collective-permute-start(bf16[896,384]{1,0:T(8,128)(2,1)} %dynamic-slice_convert_fusion.2), channel_id=1, source_target_pairs={{0,16},{1,17},{2,18},{3,19},{4,20},{5,21},{6,22},{7,23},{8,9},{9,8... | collective-permute-start | bytes 2064392 | tf_op jit(solution)/shard_map/ppermute | solution.py:585
  161.2 47.0 %collective-permute-start = (bf16[240,384]{1,0:T(8,128)(2,1)}, bf16[240,384]{1,0:T(8,128)(2,1)}, u32[]{:S(2)}, u32[]{:S(2)}) collective-permute-start(bf16[240,384]{1,0:T(8,128)(2,1)} %fusion.4), channel_id=1, source_target_pairs={{0,8},{8,0},{16,24},{24,16},{1,9},{9,1},{17,25},{25,17},{2,10},{10... | collective-permute-start | bytes 552968 | tf_op jit(solution)/shard_map/ppermute | solution.py:604
  165.4 6.8 %collective-permute-start.5 = (bf16[256,384]{1,0:T(8,128)(2,1)S(1)}, bf16[256,384]{1,0:T(8,128)(2,1)S(1)}, u32[]{:S(2)}, u32[]{:S(2)}) collective-permute-start(bf16[256,384]{1,0:T(8,128)(2,1)S(1)} %dynamic-slice_convert_fusion.5), channel_id=1, source_target_pairs={{0,1},{1,0},{2,3},{3,2},{4,5},{5,4},{6,7},{7,6},{8,24},{9,25},{10,... | collective-permute-start | bytes 589832 | tf_op jit(solution)/shard_map/ppermute | solution.py:585
  170.9 6.5 %collective-permute-start.15 = (bf16[448,384]{1,0:T(8,128)(2,1)S(1)}, bf16[448,384]{1,0:T(8,128)(2,1)S(1)}, u32[]{:S(2)}, u32[]{:S(2)}) collective-permute-start(bf16[448,384]{1,0:T(8,128)(2,1)S(1)} %dynamic-slice_convert_fusion.4), channel_id=1, source_target_pairs={{0,1},{1,0},{2,3},{3,2},{4,5},{5,4},{6,7},{7,6},{8,24},{9,25},{10,... | collective-permute-start | bytes 1032200 | tf_op jit(solution)/shard_map/ppermute | solution.py:585
  172.3 6.6 %collective-permute-start.6 = (bf16[128,384]{1,0:T(8,128)(2,1)S(1)}, bf16[128,384]{1,0:T(8,128)(2,1)S(1)}, u32[]{:S(2)}, u32[]{:S(2)}) collective-permute-start(bf16[128,384]{1,0:T(8,128)(2,1)S(1)} %dynamic-slice_convert_fusion.7), channel_id=1, source_target_pairs={{0,2},{1,3},{2,0},{3,1},{4,6},{5,7},{6,4},{7,5},{8,10},{9,11},{10,... | collective-permute-start | bytes 294920 | tf_op jit(solution)/shard_map/ppermute | solution.py:585
  177.5 4.3 %collective-permute-start.16 = (bf16[224,384]{1,0:T(8,128)(2,1)S(1)}, bf16[224,384]{1,0:T(8,128)(2,1)S(1)}, u32[]{:S(2)}, u32[]{:S(2)}) collective-permute-start(bf16[224,384]{1,0:T(8,128)(2,1)S(1)} %dynamic-slice_convert_fusion.6), channel_id=1, source_target_pairs={{0,2},{1,3},{2,0},{3,1},{4,6},{5,7},{6,4},{7,5},{8,10},{9,11},{10,... | collective-permute-start | bytes 516104 | tf_op jit(solution)/shard_map/ppermute | solution.py:585
  178.9 5.3 %collective-permute-start.7 = (bf16[64,384]{1,0:T(8,128)(2,1)S(1)}, bf16[64,384]{1,0:T(8,128)(2,1)S(1)}, u32[]{:S(2)}, u32[]{:S(2)}) collective-permute-start(bf16[64,384]{1,0:T(8,128)(2,1)S(1)} %dynamic-slice_convert_fusion.9), channel_id=1, source_target_pairs={{0,4},{1,5},{2,6},{3,7},{4,0},{5,1},{6,2},{7,3},{8,12},{9,13},{10,... | collective-permute-start | bytes 147464 | tf_op jit(solution)/shard_map/ppermute | solution.py:585
  181.9 4.4 %collective-permute-start.17 = (bf16[112,384]{1,0:T(8,128)(2,1)S(1)}, bf16[112,384]{1,0:T(8,128)(2,1)S(1)}, u32[]{:S(2)}, u32[]{:S(2)}) collective-permute-start(bf16[112,384]{1,0:T(8,128)(2,1)S(1)} %dynamic-slice_convert_fusion.8), channel_id=1, source_target_pairs={{0,4},{1,5},{2,6},{3,7},{4,0},{5,1},{6,2},{7,3},{8,12},{9,13},{10,... | collective-permute-start | bytes 258056 | tf_op jit(solution)/shard_map/ppermute | solution.py:585
  184.2 5.0 %collective-permute-start.8 = (bf16[64,384]{1,0:T(8,128)(2,1)S(1)}, bf16[64,384]{1,0:T(8,128)(2,1)S(1)}, u32[]{:S(2)}, u32[]{:S(2)}) collective-permute-start(bf16[64,384]{1,0:T(8,128)(2,1)S(1)} %add_convert_fusion.2), channel_id=1, source_target_pairs={{0,4},{1,5},{2,6},{3,7},{4,0},{5,1},{6,2},{7,3},{8,12},{9,13},{10,... | collective-permute-start | bytes 147464 | tf_op jit(solution)/shard_map/ppermute | solution.py:589
  186.3 6.1 %collective-permute-start.18 = (bf16[112,384]{1,0:T(8,128)(2,1)S(1)}, bf16[112,384]{1,0:T(8,128)(2,1)S(1)}, u32[]{:S(2)}, u32[]{:S(2)}) collective-permute-start(bf16[112,384]{1,0:T(8,128)(2,1)S(1)} %add_convert_fusion.1), channel_id=1, source_target_pairs={{0,4},{1,5},{2,6},{3,7},{4,0},{5,1},{6,2},{7,3},{8,12},{9,13},{10,... | collective-permute-start | bytes 258056 | tf_op jit(solution)/shard_map/ppermute | solution.py:589
  189.3 7.3 %collective-permute-start.9 = (bf16[128,384]{1,0:T(8,128)(2,1)S(1)}, bf16[128,384]{1,0:T(8,128)(2,1)S(1)}, u32[]{:S(2)}, u32[]{:S(2)}) collective-permute-start(bf16[128,384]{1,0:T(8,128)(2,1)S(1)} %maximum_select_fusion.9), channel_id=1, source_target_pairs={{0,2},{1,3},{2,0},{3,1},{4,6},{5,7},{6,4},{7,5},{8,10},{9,11},{10,... | collective-permute-start | bytes 294920 | tf_op jit(solution)/shard_map/ppermute | solution.py:589
  192.4 6.2 %collective-permute-start.19 = (bf16[224,384]{1,0:T(8,128)(2,1)S(1)}, bf16[224,384]{1,0:T(8,128)(2,1)S(1)}, u32[]{:S(2)}, u32[]{:S(2)}) collective-permute-start(bf16[224,384]{1,0:T(8,128)(2,1)S(1)} %maximum_select_fusion.8), channel_id=1, source_target_pairs={{0,2},{1,3},{2,0},{3,1},{4,6},{5,7},{6,4},{7,5},{8,10},{9,11},{10,... | collective-permute-start | bytes 516104 | tf_op jit(solution)/shard_map/ppermute | solution.py:589
  196.6 4.9 %collective-permute-start.10 = (bf16[256,384]{1,0:T(8,128)(2,1)S(1)}, bf16[256,384]{1,0:T(8,128)(2,1)S(1)}, u32[]{:S(2)}, u32[]{:S(2)}) collective-permute-start(bf16[256,384]{1,0:T(8,128)(2,1)S(1)} %maximum_select_fusion.7), channel_id=1, source_target_pairs={{0,1},{1,0},{2,3},{3,2},{4,5},{5,4},{6,7},{7,6},{8,24},{9,25},{10,... | collective-permute-start | bytes 589832 | tf_op jit(solution)/shard_map/ppermute | solution.py:589
  198.7 6.5 %collective-permute-start.20 = (bf16[448,384]{1,0:T(8,128)(2,1)S(1)}, bf16[448,384]{1,0:T(8,128)(2,1)}, u32[]{:S(2)}, u32[]{:S(2)}) collective-permute-start(bf16[448,384]{1,0:T(8,128)(2,1)S(1)} %maximum_select_fusion.6), channel_id=1, source_target_pairs={{0,1},{1,0},{2,3},{3,2},{4,5},{5,4},{6,7},{7,6},{8,24},{9,25},{10,... | collective-permute-start | bytes 1032200 | tf_op jit(solution)/shard_map/ppermute | solution.py:589
  201.6 8.4 %collective-permute-start.11 = (bf16[512,384]{1,0:T(8,128)(2,1)S(1)}, bf16[512,384]{1,0:T(8,128)(2,1)}, u32[]{:S(2)}, u32[]{:S(2)}) collective-permute-start(bf16[512,384]{1,0:T(8,128)(2,1)S(1)} %maximum_select_fusion.5), channel_id=1, source_target_pairs={{0,16},{1,17},{2,18},{3,19},{4,20},{5,21},{6,22},{7,23},{8,9},{9,8... | collective-permute-start | bytes 1179656 | tf_op jit(solution)/shard_map/ppermute | solution.py:589
  206.6 27.1 %collective-permute-start.21 = (bf16[896,384]{1,0:T(8,128)(2,1)S(1)}, bf16[896,384]{1,0:T(8,128)(2,1)}, u32[]{:S(2)}, u32[]{:S(2)}) collective-permute-start(bf16[896,384]{1,0:T(8,128)(2,1)S(1)} %maximum_select_fusion.4), channel_id=1, source_target_pairs={{0,16},{1,17},{2,18},{3,19},{4,20},{5,21},{6,22},{7,23},{8,9},{9,8... | collective-permute-start | bytes 2064392 | tf_op jit(solution)/shard_map/ppermute | solution.py:589
  209.2 20.2 %collective-permute-start.1 = (bf16[240,384]{1,0:T(8,128)(2,1)S(1)}, bf16[240,384]{1,0:T(8,128)(2,1)S(1)}, u32[]{:S(2)}, u32[]{:S(2)}) collective-permute-start(bf16[240,384]{1,0:T(8,128)(2,1)S(1)} %fusion.3), channel_id=1, source_target_pairs={{0,16},{16,0},{8,24},{24,8},{1,17},{17,1},{9,25},{25,9},{2,18},{18... | collective-permute-start | bytes 552968 | tf_op jit(solution)/shard_map/ppermute | solution.py:605
  211.4 26.7 %copy-start.3 = (bf16[1024,384]{1,0:T(8,128)(2,1)}, bf16[1024,384]{1,0:T(8,128)(2,1)S(1)}, u32[]{:S(2)}) copy-start(bf16[1024,384]{1,0:T(8,128)(2,1)S(1)} %maximum_select_fusion.3) | copy-start | bytes 2359300
  211.4 29.3 %collective-permute-start.12 = (bf16[1024,384]{1,0:T(8,128)(2,1)S(1)}, bf16[1024,384]{1,0:T(8,128)(2,1)}, u32[]{:S(2)}, u32[]{:S(2)}) collective-permute-start(bf16[1024,384]{1,0:T(8,128)(2,1)S(1)} %maximum_select_fusion.3), channel_id=1, source_target_pairs={{0,8},{1,9},{2,10},{3,11},{4,12},{5,13},{6,14},{7,15},{8,0},{9,1},... | collective-permute-start | bytes 2359304 | tf_op jit(solution)/shard_map/ppermute | solution.py:589
  229.5 6.9 %collective-permute-start.2 = (bf16[240,384]{1,0:T(8,128)(2,1)S(1)}, bf16[240,384]{1,0:T(8,128)(2,1)S(1)}, u32[]{:S(2)}, u32[]{:S(2)}) collective-permute-start(bf16[240,384]{1,0:T(8,128)(2,1)S(1)} %add_convert_fusion), channel_id=1, source_target_pairs={{0,8},{8,0},{16,24},{24,16},{1,9},{9,1},{17,25},{25,17},{2,10},{10... | collective-permute-start | bytes 552968 | tf_op jit(solution)/shard_map/ppermute | solution.py:607
  236.4 12.9 %collective-permute-start.22 = (bf16[1792,384]{1,0:T(8,128)(2,1)}, bf16[1792,384]{1,0:T(8,128)(2,1)}, u32[]{:S(2)}, u32[]{:S(2)}) collective-permute-start(bf16[1792,384]{1,0:T(8,128)(2,1)} %maximum_select_fusion.2), channel_id=1, source_target_pairs={{0,8},{1,9},{2,10},{3,11},{4,12},{5,13},{6,14},{7,15},{8,0},{9,1},... | collective-permute-start | bytes 4128776 | tf_op jit(solution)/shard_map/ppermute | solution.py:589
  (6 other events, 92.4 us)

commit v2 on v1

v2 whole, which is shorter than its diff:
```python
import functools

import jax
import jax.numpy as jnp
import numpy as np
from jax import lax
from jax.experimental import pallas as pl
from jax.experimental.pallas import tpu as pltpu
from jax.sharding import PartitionSpec as P

D = 384
HEADS = 6
HEAD = 64
PAIRS = 3
PAIR = 128
FF = 1536
DIN = 768
SLOT = 160
LEN = 1568
STEP = 112
BLOCK = 256
BLOCKS = FF // BLOCK
FC_USED = 10392
QKV_USED = 5784
AXES = ("seq", "clip")
VMEM = 60 * 1024 * 1024

bf16 = jnp.bfloat16
f32 = jnp.float32


def dot(left, right):
    return lax.dot_general(
        left, right, (((1,), (0,)), ((), ())), preferred_element_type=f32
    )


def dot_rt(left, right):
    return lax.dot_general(
        left, right, (((1,), (1,)), ((), ())), preferred_element_type=f32
    )


def dot_lt(left, right):
    return lax.dot_general(
        left, right, (((0,), (0,)), ((), ())), preferred_element_type=f32
    )


def split3(value):
    high = value.astype(bf16)
    rest = value - high.astype(f32)
    middle = rest.astype(bf16)
    low = (rest - middle.astype(f32)).astype(bf16)
    return high, middle, low


def sinusoid_table(length, columns):
    positions = np.arange(length, dtype=np.float64)[:, None]
    column = np.arange(columns)
    angles = positions / np.power(10000.0, (2 * (column // 2)) / columns)[None, :]
    return np.where((column % 2)[None, :] == 0, np.sin(angles), np.cos(angles)).astype(np.float32)


def own_lanes(head):
    lane = lax.broadcasted_iota(jnp.int32, (1, PAIR), 1)
    return (lane < HEAD) if head == 0 else (lane >= HEAD)


def column_sums(value):
    return jnp.sum(value, axis=0, keepdims=True)


def square_sum(weight):
    columns = weight.shape[1]
    total = column_sums(weight.astype(f32) ** 2)
    result = total[:, :PAIR]
    for first in range(PAIR, columns, PAIR):
        result = result + total[:, first : first + PAIR]
    return result


def lane_mean(value):
    return jnp.mean(value, axis=1, keepdims=True)


def forward_kernel(
    start_ref,
    x_ref,
    pos_ref,
    table_ref,
    w_proj_ref,
    b_proj_ref,
    mask_ref,
    gain1_ref,
    bias1_ref,
    w_qkv_ref,
    q_bias_ref,
    v_bias_ref,
    w_out_ref,
    b_out_ref,
    gain2_ref,
    bias2_ref,
    w_fc1_ref,
    b_fc1_ref,
    w_fc2_ref,
    b_fc2_ref,
    cot_ref,
    out_ref,
    gs_ref,
    extra_ref,
    gmid_ref,
    kept_ref,
    sent_ref,
    norms_ref,
    p_hbm,
    q_hbm,
    k_hbm,
    v_hbm,
    normed_hbm,
    xhat_hbm,
    rstd_hbm,
    p_s,
    q_s,
    k_s,
    v_s,
    normed_s,
    xhat_s,
    rstd_s,
    emb_s,
    own_s,
    att_s,
    linv_s,
    attended_s,
    middle_s,
    xhat2_s,
    rstd2_s,
    normed2_s,
    gn_s,
    vec_s,
    flat_s,
    sems,
    p_sems,
    *,
    rows,
    clips,
):
    step = pl.program_id(0)
    per = PAIRS + 1
    clip = jnp.minimum(lax.div(step, per), clips - 1)
    phase = step - clip * per
    half = kept_ref.shape[0]

    def saves(number):
        pairs = [
            (q_s, q_hbm),
            (k_s, k_hbm),
            (v_s, v_hbm),
            (normed_s, normed_hbm),
            (xhat_s, xhat_hbm),
            (rstd_s, rstd_hbm),
        ]
        return [
            pltpu.make_async_copy(source, target.at[number], sems.at[index])
            for index, (source, target) in enumerate(pairs)
        ]

    def p_save(number):
        slot = lax.rem(number, 2)
        at = lax.div(number, PAIRS)
        pair = lax.rem(number, PAIRS)
        return pltpu.make_async_copy(
            p_s.at[slot], p_hbm.at[at, pl.ds(2 * pair, 2)], p_sems.at[slot]
        )

    @pl.when(phase == 0)
    def _():
        @pl.when(clip > 0)
        def _():
            for copy in saves(clip - 1):
                copy.wait()

        projected = dot(x_ref[0], w_proj_ref[...]) + b_proj_ref[...][None, :]
        high, middle, low = split3(projected - mask_ref[...][None, :])
        row = lax.broadcasted_iota(jnp.int32, (LEN, 1), 0)
        onehot = (row == pos_ref[0]).astype(f32).astype(bf16)
        emb_s[...] = (
            (table_ref[...].reshape(LEN, D) + mask_ref[...][None, :])
            + dot(onehot, low)
            + dot(onehot, middle)
        ) + dot(onehot, high)

        def norm_rows(number, carry):
            at = pl.ds(pl.multiple_of(number * STEP, STEP), STEP)
            value = emb_s[at, :]
            centered = value - lane_mean(value)
            rstd = lax.rsqrt(lane_mean(centered * centered) + 1e-05)
            xhat = centered * rstd
            xhat_s[at, :] = xhat.astype(bf16)
            normed_s[at, :] = (xhat * gain1_ref[...][None, :] + bias1_ref[...][None, :]).astype(
                bf16
            )
            rstd_s[at, :] = rstd
            return carry

        lax.fori_loop(0, LEN // STEP, norm_rows, 0)
        own_s[pl.ds(pl.multiple_of(clip * rows, 8), rows), :] = emb_s[:rows, :]
        normed = normed_s[...]
        k_s[...] = dot(normed, w_qkv_ref[:, D : 2 * D]).astype(bf16)
        v_s[...] = (dot(normed, w_qkv_ref[:, 2 * D :]) + v_bias_ref[...][None, :]).astype(bf16)
        q_s[...] = (dot(normed[:rows], w_qkv_ref[:, :D]) + q_bias_ref[...][None, :]).astype(bf16)
        for copy in saves(clip):
            copy.start()

        @pl.when(clip == 0)
        def _():
            norms_ref[0:1, :] = square_sum(w_proj_ref[...])
            norms_ref[1:2, :] = square_sum(w_out_ref[...])
            norms_ref[2:4, :] = jnp.zeros((2, PAIR), f32)
            norms_ref[4:5, :] = square_sum(w_qkv_ref[...])

    @pl.when(jnp.logical_and(phase >= 1, phase < per))
    def _():
        number = clip * PAIRS + phase - 1
        slot = lax.rem(number, 2)

        @pl.when(number >= 2)
        def _():
            p_save(number - 2).wait()

        at = pl.ds(pl.multiple_of((phase - 1) * PAIR, PAIR), PAIR)
        query = q_s[:, at]
        key = k_s[:, at]
        value = jnp.concatenate([v_s[:, at], jnp.ones((LEN, PAIR), bf16)], axis=1)
        parts = []
        for head in range(2):
            scores = dot_rt(jnp.where(own_lanes(head), query, jnp.zeros_like(query)), key)
            largest = jnp.max(scores, axis=1, keepdims=True)
            weights = jnp.exp2((scores - largest) * (HEAD**-0.5 * np.log2(np.e))).astype(bf16)
            p_s[slot, head] = weights
            parts.append(dot(weights, value))
        first = own_lanes(0)
        inverse = 1.0 / jnp.where(first, parts[0][:, PAIR:], parts[1][:, PAIR:])
        group = pl.ds(pl.multiple_of(clip * rows, 8), rows)
        linv_s[group, at] = inverse
        att_s[group, at] = jnp.where(first, parts[0][:, :PAIR], parts[1][:, :PAIR]) * inverse
        p_save(number).start()

    @pl.when(step == clips * per)
    def _():
        for copy in saves(clips - 1):
            copy.wait()
        p_save(clips * PAIRS - 2).wait()
        p_save(clips * PAIRS - 1).wait()
        attended = att_s[...].astype(bf16)
        attended_s[...] = attended
        middle = own_s[...] + (dot(attended, w_out_ref[...]) + b_out_ref[...][None, :])
        centered = middle - lane_mean(middle)
        rstd = lax.rsqrt(lane_mean(centered * centered) + 1e-05)
        xhat = centered * rstd
        xhat2_s[...] = xhat
        rstd2_s[...] = rstd
        normed2_s[...] = (xhat * gain2_ref[...][None, :] + bias2_ref[...][None, :]).astype(bf16)
        middle_s[...] = middle + b_fc2_ref[...][None, :]
        gn_s[...] = jnp.zeros_like(gn_s)
        flat_s[FC_USED - 24 :, :] = jnp.zeros_like(flat_s[FC_USED - 24 :, :])

    @pl.when(step >= clips * per)
    def _():
        block = step - clips * per
        normed2 = normed2_s[...]
        cot = cot_ref[...]
        w_fc1 = w_fc1_ref[...]
        w_fc2 = w_fc2_ref[...]
        norms_ref[2:3, :] += square_sum(w_fc1)
        norms_ref[3:4, :] += square_sum(w_fc2)
        pre = dot(normed2, w_fc1) + b_fc1_ref[...][None, :]
        cdf = 0.5 + 0.5 * lax.erf(pre * np.float32(0.5**0.5))
        hidden = (pre * cdf).astype(bf16)
        slope = cdf + pre * (
            jnp.exp2(pre * pre * (-0.5 * np.log2(np.e))) * ((2 * np.pi) ** -0.5)
        )
        grad_pre = dot_rt(cot, w_fc2) * slope
        grad_pre_b = grad_pre.astype(bf16)
        middle_s[...] += dot(hidden, w_fc2)
        gn_s[...] += dot_rt(grad_pre_b, w_fc1)
        grad_w2 = dot_lt(hidden, cot).astype(bf16)
        for column in range(D // PAIR):
            first = FF * PAIRS + column * FF + block * BLOCK
            flat_s[pl.ds(pl.multiple_of(first, 16), BLOCK), :] = grad_w2[
                :, column * PAIR : (column + 1) * PAIR
            ]
        grad_w1 = dot_lt(normed2, grad_pre_b).astype(bf16)
        sums = column_sums(grad_pre_b.astype(f32))
        for piece in range(BLOCK // PAIR):
            lanes = slice(piece * PAIR, (piece + 1) * PAIR)
            number = block * (BLOCK // PAIR) + piece
            flat_s[pl.ds(pl.multiple_of(number * D, 16), D), :] = grad_w1[:, lanes]
            row = 8 * lax.rem(number, PAIRS) + lax.div(number, PAIRS)
            vec_s[pl.ds(row, 1), :] = sums[:, lanes]

    @pl.when(step == clips * per + BLOCKS - 1)
    def _():
        out_ref[...] = middle_s[...].astype(bf16)
        cot_f = cot_ref[...].astype(f32)
        grad_normed = gn_s[...]
        xhat = xhat2_s[...]
        scaled = grad_normed * gain2_ref[...][None, :]
        grad_middle = cot_f + rstd2_s[...] * (
            scaled - lane_mean(scaled) - xhat * lane_mean(scaled * xhat)
        )
        gmid_ref[...] = grad_middle
        grad_branch = grad_middle.astype(bf16)
        vectors = [
            column_sums(cot_f),
            column_sums(grad_normed * xhat),
            column_sums(grad_normed),
            column_sums(grad_branch.astype(f32)),
        ]
        grad_out = dot_lt(attended_s[...], grad_branch).astype(bf16)
        for column in range(D // PAIR):
            lanes = slice(column * PAIR, (column + 1) * PAIR)
            first = 2 * FF * PAIRS + column * D
            flat_s[first : first + D, :] = grad_out[:, lanes]
            for number, vector in enumerate(vectors):
                row = 8 * column + 4 + number
                vec_s[row : row + 1, :] = vector[:, lanes]
        flat_s[FC_USED - 24 : FC_USED, :] = vec_s[...].astype(bf16)
        bit = start_ref[1]
        kept_ref[...] = flat_s[pl.ds(pl.multiple_of(bit * half, 16), half), :]
        sent_ref[...] = flat_s[pl.ds(pl.multiple_of((1 - bit) * half, 16), half), :]
        grad_att = dot_rt(grad_branch, w_out_ref[...]).astype(bf16).astype(f32)
        grad_s = (grad_att * linv_s[...]).astype(bf16)
        gs_ref[...] = grad_s
        product = grad_s.astype(f32) * att_s[...]
        lane = lax.broadcasted_iota(jnp.int32, (1, PAIR), 1)
        packed = jnp.zeros((clips * rows, PAIR), f32)
        for pair in range(PAIRS):
            piece = product[:, pair * PAIR : (pair + 1) * PAIR]
            for head in range(2):
                inner = -jnp.sum(
                    jnp.where(own_lanes(head), piece, 0.0), axis=1, keepdims=True
                )
                for index, term in enumerate(split3(inner)):
                    at = 3 * (2 * pair + head) + index
                    packed = jnp.where(lane == at, term.astype(f32), packed)
        extra_ref[...] = packed.astype(bf16)


def backward_kernel(
    start_ref,
    q_ref,
    k_ref,
    v_ref,
    gs_ref,
    extra_ref,
    p_ref,
    x_ref,
    pos_ref,
    w_qkv_ref,
    gain1_ref,
    normed_hbm,
    xhat_hbm,
    rstd_hbm,
    gmid_hbm,
    *rest,
    rows,
    base,
    count,
    last,
):
    if last:
        acc_hbm, kept_ref, sent_ref, proj_kept_ref, proj_sent_ref = rest[:5]
        acc_s, total_sem = rest[5:7]
        scratch = rest[7:]
    else:
        acc_s, proj_kept_ref, proj_sent_ref = rest[:3]
        scratch = rest[3:]
    (normed_s, xhat_s, rstd_s, own_s, dq_s, dkv_s, gn_s, high_s, low_s, proj_s, sems) = scratch
    per = PAIRS + 1
    step = pl.program_id(0)
    clip = lax.div(step, per)
    phase = step - clip * per
    lane = lax.broadcasted_iota(jnp.int32, (1, PAIR), 1)

    def loads():
        at = base + clip
        pairs = [
            (normed_hbm.at[at], normed_s),
            (xhat_hbm.at[at], xhat_s),
            (rstd_hbm.at[at], rstd_s),
            (gmid_hbm.at[pl.ds(pl.multiple_of(at * rows, 8), rows)], own_s.at[pl.ds(0, rows)]),
        ]
        return [
            pltpu.make_async_copy(source, target, sems.at[index])
            for index, (source, target) in enumerate(pairs)
        ]

    @pl.when(phase == 0)
    def _():
        for copy in loads():
            copy.start()

    @pl.when(step == 0)
    def _():
        own_s[rows:, :] = jnp.zeros_like(own_s[rows:, :])
        if last:
            pltpu.make_async_copy(acc_hbm, acc_s, total_sem).start()
        else:
            acc_s[...] = jnp.zeros_like(acc_s)

    @pl.when(phase < PAIRS)
    def _():
        at = pl.ds(pl.multiple_of(phase * PAIR, PAIR), PAIR)
        query = q_ref[0, :, at] * jnp.asarray(HEAD**-0.5, bf16)
        key = k_ref[0, :, at]
        value = jnp.concatenate([v_ref[0, :, at], jnp.ones((LEN, PAIR), bf16)], axis=1)
        grad = gs_ref[:, at]
        extra = extra_ref[...]
        queries, keys, values = [], [], []
        for head in range(2):
            first = 3 * (2 * phase + head)
            inner = jnp.logical_and(lane >= first, lane < first + 3)
            left = jnp.concatenate(
                [
                    jnp.where(own_lanes(head), grad, jnp.zeros_like(grad)),
                    jnp.where(inner, extra, jnp.zeros_like(extra)),
                ],
                axis=1,
            )
            weights = p_ref[0, head]
            grad_scores = (weights.astype(f32) * dot_rt(left, value)).astype(bf16)
            queries.append(dot(grad_scores, key))
            keys.append(dot_lt(grad_scores, query))
            values.append(dot_lt(weights, grad))
        side = own_lanes(0)
        dq_s[:, at] = (jnp.where(side, queries[0], queries[1]) * (HEAD**-0.5)).astype(bf16)
        dkv_s[:, at] = jnp.where(side, keys[0], keys[1]).astype(bf16)
        at = pl.ds(pl.multiple_of(phase * PAIR + D, PAIR), PAIR)
        dkv_s[:, at] = jnp.where(side, values[0], values[1]).astype(bf16)

    @pl.when(phase == PAIRS)
    def _():
        for copy in loads():
            copy.wait()
        if last:
            @pl.when(step == PAIRS)
            def _():
                pltpu.make_async_copy(acc_hbm, acc_s, total_sem).wait()

        normed = normed_s[...]
        grad_q = dq_s[...]
        grad_kv = dkv_s[...]
        gn_s[...] = dot_rt(grad_kv, w_qkv_ref[:, D:])
        gn_s[:rows, :] += dot_rt(grad_q, w_qkv_ref[:, :D])
        part_q = dot_lt(normed[:rows], grad_q)
        part_kv = dot_lt(normed, grad_kv)
        for index in range(PAIRS):
            acc_s[index * D : (index + 1) * D, :] += part_q[:, index * PAIR : (index + 1) * PAIR]
        for index in range(2 * PAIRS):
            first = (PAIRS + index) * D
            acc_s[first : first + D, :] += part_kv[:, index * PAIR : (index + 1) * PAIR]
        ones = jnp.ones((8, LEN), bf16)
        sum_q = dot(ones[:, :rows], grad_q)[:1]
        sum_v = dot(ones, grad_kv[:, D:])[:1]

        def norm_rows(number, carry, with_own):
            at = pl.ds(pl.multiple_of(number * STEP, STEP), STEP)
            sum_gain, sum_bias, sum_emb = carry
            value = gn_s[at, :]
            xhat = xhat_s[at, :].astype(f32)
            sum_bias = sum_bias + column_sums(value)
            sum_gain = sum_gain + column_sums(value * xhat)
            scaled = value * gain1_ref[...][None, :]
            grad = rstd_s[at, :] * (
                scaled - lane_mean(scaled) - xhat * lane_mean(scaled * xhat)
            )
            if with_own:
                grad = grad + own_s[at, :]
            sum_emb = sum_emb + column_sums(grad)
            high = grad.astype(bf16)
            high_s[at, :] = high
            low_s[at, :] = (grad - high.astype(f32)).astype(bf16)
            return sum_gain, sum_bias, sum_emb

        zero = jnp.zeros((1, D), f32)
        own_steps = own_s.shape[0] // STEP
        carry = lax.fori_loop(
            0, own_steps, functools.partial(norm_rows, with_own=True), (zero, zero, zero)
        )
        sum_gain, sum_bias, sum_emb = lax.fori_loop(
            own_steps, LEN // STEP, functools.partial(norm_rows, with_own=False), carry
        )
        column = lax.broadcasted_iota(jnp.int32, (1, LEN), 1)
        onehot = (pos_ref[0] == column).astype(f32).astype(bf16)
        grad_proj = dot(onehot, high_s[...]) + dot(onehot, low_s[...])
        proj_s[...] = grad_proj
        bit = start_ref[1]
        part = SLOT // 2
        proj_kept_ref[0] = proj_s[pl.ds(pl.multiple_of(bit * part, 8), part), :]
        proj_sent_ref[0] = proj_s[
            pl.ds(pl.multiple_of((1 - bit) * part, 8), part), :
        ].astype(bf16)
        sum_proj = column_sums(grad_proj)
        vectors = [sum_proj, sum_emb - sum_proj, sum_gain, sum_bias, sum_q, sum_v]
        weight = dot_lt(x_ref[0], grad_proj[: x_ref.shape[1]].astype(bf16))
        for index in range(D // PAIR):
            lanes = slice(index * PAIR, (index + 1) * PAIR)
            first = 3 * PAIRS * D + index * DIN
            acc_s[first : first + DIN, :] += weight[:, lanes]
            first = 3 * PAIRS * D + PAIRS * DIN + 8 * index
            for number, vector in enumerate(vectors):
                acc_s[first + number : first + number + 1, :] += vector[:, lanes]

    if last:

        @pl.when(step == count * per - 1)
        def _():
            bit = start_ref[1]
            half = kept_ref.shape[0]
            kept_ref[...] = acc_s[pl.ds(pl.multiple_of(bit * half, 8), half), :]
            sent_ref[...] = acc_s[pl.ds(pl.multiple_of((1 - bit) * half, 8), half), :].astype(
                bf16
            )


def place(target, lanes, source, parts, total):
    for side, where, at, size in parts:
        value = source(side, where, size).astype(f32)
        target[at : at + size, lanes] = value
        if total is not None:
            square = jnp.sum((value * value).reshape(size // 8, 8, PAIR), axis=0)
            total = square if total is False else total + square
    return total


def split_rows(first, count, half):
    result = []
    done = 0
    while done < count:
        side, inside = divmod(first + done, half)
        length = min(count - done, half - inside)
        result.append((side, inside, done, length))
        done += length
    return result


def lanes_of(index):
    return slice(index * PAIR, (index + 1) * PAIR)


def whole_mean(total, size):
    value = jnp.sum(jnp.sum(total, axis=1, keepdims=True), axis=0, keepdims=True)
    return value / size


def assemble_fc_kernel(
    start_ref,
    mine_ref,
    other_ref,
    w_out_ref,
    w_fc1_ref,
    w_fc2_ref,
    b_out_ref,
    gain_ref,
    bias_ref,
    b_fc1_ref,
    b_fc2_ref,
    mean_ref,
):
    half = mine_ref.shape[0]

    def body(halves):
        def source(side, where, size):
            return halves[side][where : where + size, :]

        total = False
        for index in range(PAIRS):
            parts = split_rows(2 * FF * PAIRS + index * D, D, half)
            total = place(w_out_ref, lanes_of(index), source, parts, total)
        mean_out = whole_mean(total, D * D)
        total = False
        for index in range(FF // PAIR):
            parts = split_rows(index * D, D, half)
            total = place(w_fc1_ref, lanes_of(index), source, parts, total)
        mean_fc1 = whole_mean(total, D * FF)
        total = False
        for index in range(PAIRS):
            parts = split_rows(FF * PAIRS + index * FF, FF, half)
            total = place(w_fc2_ref, lanes_of(index), source, parts, total)
        mean_fc2 = whole_mean(total, FF * D)
        first = 2 * FF * PAIRS + PAIRS * D - half
        vectors = source(1, first, 24).astype(f32)
        for index in range(PAIRS):
            lanes = lanes_of(index)
            for number in range(4):
                b_fc1_ref[number * D + index * PAIR : number * D + (index + 1) * PAIR] = vectors[
                    8 * index + number
                ]
            for number, target in enumerate([b_fc2_ref, gain_ref, bias_ref, b_out_ref]):
                target[lanes] = vectors[8 * index + 4 + number]
        row = lax.broadcasted_iota(jnp.int32, (8, PAIR), 0)
        mean_ref[...] = jnp.where(
            row == 1, mean_out, jnp.where(row == 2, mean_fc1, mean_fc2)
        )

    bit = start_ref[1]

    @pl.when(bit == 0)
    def _():
        body((mine_ref, other_ref))

    @pl.when(bit == 1)
    def _():
        body((other_ref, mine_ref))


def assemble_qkv_kernel(
    start_ref,
    mine_ref,
    other_ref,
    norms_ref,
    mean_ref,
    w_proj_ref,
    w_qkv_ref,
    b_proj_ref,
    mask_ref,
    gain_ref,
    bias_ref,
    q_bias_ref,
    v_bias_ref,
    trust_ref,
    trust_qkv_ref,
):
    half = mine_ref.shape[0]

    def body(halves):
        def source(side, where, size):
            return halves[side][where : where + size, :]

        total = False
        for index in range(PAIRS):
            parts = split_rows(3 * PAIRS * D + index * DIN, DIN, half)
            total = place(w_proj_ref, lanes_of(index), source, parts, total)
        mean_proj = whole_mean(total, DIN * D)
        total = False
        for index in range(3 * PAIRS):
            parts = split_rows(index * D, D, half)
            total = place(w_qkv_ref, lanes_of(index), source, parts, total)
        mean_qkv = whole_mean(total, D * 3 * D)
        vectors = source(1, 3 * PAIRS * D + PAIRS * DIN - half, 24).astype(f32)
        targets = [b_proj_ref, mask_ref, gain_ref, bias_ref, q_bias_ref, v_bias_ref]
        for index in range(PAIRS):
            for number, target in enumerate(targets):
                target[lanes_of(index)] = vectors[8 * index + number]
        lane = lax.broadcasted_iota(jnp.int32, (1, PAIR), 1)
        means = [mean_proj, mean_ref[1:2], mean_ref[2:3], mean_ref[3:4], mean_qkv]
        sums = jnp.sum(norms_ref[...], axis=1, keepdims=True)
        sizes = [DIN * D, D * D, D * FF, FF * D, D * 3 * D]
        grads = jnp.ones((1, PAIR), f32)
        weights = jnp.ones((1, PAIR), f32)
        for index, (mean, size) in enumerate(zip(means, sizes)):
            grads = jnp.where(lane == index, mean, grads)
            weights = jnp.where(lane == index, sums[index : index + 1] / size, weights)
        ratios = jnp.sqrt(weights) / jnp.sqrt(grads + 1e-06)
        trust_ref[...] = ratios[0, :4]
        trust_qkv_ref[...] = ratios[0, 4:5]

    bit = start_ref[1]

    @pl.when(bit == 0)
    def _():
        body((mine_ref, other_ref))

    @pl.when(bit == 1)
    def _():
        body((other_ref, mine_ref))


def whole(shape):
    return pl.BlockSpec(shape, lambda i, s: (0,) * len(shape), pipeline_mode=pl.Buffered(1))


def shape_of(shape, dtype):
    return jax.ShapeDtypeStruct(shape, dtype)


def kernel_call(kernel, grid, in_specs, out_specs, out_shape, scratch, name, cost, args):
    return pl.pallas_call(
        kernel,
        grid_spec=pltpu.PrefetchScalarGridSpec(
            num_scalar_prefetch=1,
            grid=grid,
            in_specs=in_specs,
            out_specs=out_specs,
            scratch_shapes=scratch,
        ),
        out_shape=out_shape,
        compiler_params=pltpu.CompilerParams(
            dimension_semantics=("arbitrary",), vmem_limit_bytes=VMEM
        ),
        cost_estimate=pl.CostEstimate(
            flops=cost[0], bytes_accessed=cost[1], transcendentals=cost[2]
        ),
        name=name,
    )(*args)


def run_forward(start, x_vis, local_pos, table, params, cotangent, rows, half):
    clips, visible, _ = x_vis.shape
    (
        w_proj,
        b_proj,
        mask_token,
        ln1_gain,
        ln1_bias,
        w_qkv,
        q_bias,
        v_bias,
        w_out,
        b_out,
        ln2_gain,
        ln2_bias,
        w_fc1,
        b_fc1,
        w_fc2,
        b_fc2,
    ) = params
    per = PAIRS + 1
    steps = clips * per

    def clip_at(i):
        return jnp.minimum(lax.div(i, per), clips - 1)

    def block_at(i):
        return jnp.maximum(i - steps, 0)

    tokens = clips * rows
    any_space = pl.BlockSpec(memory_space=pl.ANY)
    vector = whole((D,))
    in_specs = [
        pl.BlockSpec((1, visible, DIN), lambda i, s: (clip_at(i), 0, 0)),
        pl.BlockSpec((1, 1, visible), lambda i, s: (clip_at(i), 0, 0)),
        pl.BlockSpec(
            (pl.Element(LEN // 8), pl.Element(8), pl.Element(D)), lambda i, s: (s[0], 0, 0)
        ),
        whole((DIN, D)),
        vector,
        vector,
        vector,
        vector,
        whole((D, 3 * D)),
        vector,
        vector,
        whole((D, D)),
        vector,
        vector,
        vector,
        pl.BlockSpec((D, BLOCK), lambda i, s: (0, block_at(i))),
        pl.BlockSpec((BLOCK,), lambda i, s: (block_at(i),)),
        pl.BlockSpec((BLOCK, D), lambda i, s: (block_at(i), 0)),
        vector,
        whole((tokens, D)),
    ]
    out_specs = [
        whole((tokens, D)),
        whole((tokens, D)),
        whole((tokens, PAIR)),
        whole((tokens, D)),
        whole((half, PAIR)),
        whole((half, PAIR)),
        whole((8, PAIR)),
    ] + [any_space] * 7
    out_shape = [
        shape_of((tokens, D), bf16),
        shape_of((tokens, D), bf16),
        shape_of((tokens, PAIR), bf16),
        shape_of((tokens, D), f32),
        shape_of((half, PAIR), bf16),
        shape_of((half, PAIR), bf16),
        shape_of((8, PAIR), f32),
        shape_of((clips, HEADS, rows, LEN), bf16),
        shape_of((clips, rows, D), bf16),
        shape_of((clips, LEN, D), bf16),
        shape_of((clips, LEN, D), bf16),
        shape_of((clips, LEN, D), bf16),
        shape_of((clips, LEN, D), bf16),
        shape_of((clips, LEN, 1), f32),
    ]
    scratch = [
        pltpu.VMEM((2, 2, rows, LEN), bf16),
        pltpu.VMEM((rows, D), bf16),
        pltpu.VMEM((LEN, D), bf16),
        pltpu.VMEM((LEN, D), bf16),
        pltpu.VMEM((LEN, D), bf16),
        pltpu.VMEM((LEN, D), bf16),
        pltpu.VMEM((LEN, 1), f32),
        pltpu.VMEM((LEN, D), f32),
        pltpu.VMEM((tokens, D), f32),
        pltpu.VMEM((tokens, D), f32),
        pltpu.VMEM((tokens, D), f32),
        pltpu.VMEM((tokens, D), bf16),
        pltpu.VMEM((tokens, D), f32),
        pltpu.VMEM((tokens, D), f32),
        pltpu.VMEM((tokens, 1), f32),
        pltpu.VMEM((tokens, D), bf16),
        pltpu.VMEM((tokens, D), f32),
        pltpu.VMEM((24, PAIR), f32),
        pltpu.VMEM((2 * half, PAIR), bf16),
        pltpu.SemaphoreType.DMA((6,)),
        pltpu.SemaphoreType.DMA((2,)),
    ]
    return kernel_call(
        functools.partial(forward_kernel, rows=rows, clips=clips),
        (steps + BLOCKS,),
        in_specs,
        out_specs,
        out_shape,
        scratch,
        "forward",
        (40_000_000_000, 60_000_000, 13_000_000),
        (
            start,
            x_vis,
            local_pos[:, None, :],
            table,
            w_proj,
            b_proj,
            mask_token,
            ln1_gain,
            ln1_bias,
            w_qkv,
            q_bias,
            v_bias,
            w_out,
            b_out,
            ln2_gain,
            ln2_bias,
            w_fc1,
            b_fc1,
            w_fc2,
            b_fc2,
            cotangent.reshape(tokens, D),
        ),
    )


def run_backward(start, saved, x_vis, padded_pos, w_qkv, ln1_gain, rows, half, base, count, acc):
    query, key, value, grads, extra, weights, normed, xhat, rstd, gmid = saved
    _, visible, _ = x_vis.shape
    per = PAIRS + 1
    last = acc is not None
    own_rows = -(-rows // STEP) * STEP
    any_space = pl.BlockSpec(memory_space=pl.ANY)

    def at(i):
        return base + lax.div(i, per)

    def block(*shape):
        return pl.BlockSpec((1,) + shape, lambda i, s: (at(i),) + (0,) * len(shape))

    proj_spec = pl.BlockSpec((1, SLOT // 2, D), lambda i, s: (lax.div(i, per), 0, 0))
    proj_shapes = [
        shape_of((count, SLOT // 2, D), f32),
        shape_of((count, SLOT // 2, D), bf16),
    ]
    in_specs = [
        block(rows, D),
        block(LEN, D),
        block(LEN, D),
        pl.BlockSpec((rows, D), lambda i, s: (at(i), 0)),
        pl.BlockSpec((rows, PAIR), lambda i, s: (at(i), 0)),
        pl.BlockSpec(
            (1, 2, rows, LEN),
            lambda i, s: (at(i), jnp.minimum(lax.rem(i, per), PAIRS - 1), 0, 0),
        ),
        block(visible, DIN),
        block(SLOT, 1),
        whole((D, 3 * D)),
        whole((D,)),
    ] + [any_space] * 4
    args = [
        start,
        query,
        key,
        value,
        grads,
        extra,
        weights,
        x_vis,
        padded_pos[:, :, None],
        w_qkv,
        ln1_gain,
        normed,
        xhat,
        rstd,
        gmid,
    ]
    scratch = [
        pltpu.VMEM((LEN, D), bf16),
        pltpu.VMEM((LEN, D), bf16),
        pltpu.VMEM((LEN, 1), f32),
        pltpu.VMEM((own_rows, D), f32),
        pltpu.VMEM((rows, D), bf16),
        pltpu.VMEM((LEN, 2 * D), bf16),
        pltpu.VMEM((LEN, D), f32),
        pltpu.VMEM((LEN, D), bf16),
        pltpu.VMEM((LEN, D), bf16),
        pltpu.VMEM((SLOT, D), f32),
        pltpu.SemaphoreType.DMA((4,)),
    ]
    if last:
        in_specs.append(any_space)
        args.append(acc)
        out_specs = [whole((half, PAIR)), whole((half, PAIR)), proj_spec, proj_spec]
        out_shape = [shape_of((half, PAIR), f32), shape_of((half, PAIR), bf16)] + proj_shapes
        scratch = [pltpu.VMEM((2 * half, PAIR), f32), pltpu.SemaphoreType.DMA] + scratch
    else:
        out_specs = [whole((2 * half, PAIR)), proj_spec, proj_spec]
        out_shape = [shape_of((2 * half, PAIR), f32)] + proj_shapes
    return kernel_call(
        functools.partial(backward_kernel, rows=rows, base=base, count=count, last=last),
        (count * per,),
        in_specs,
        out_specs,
        out_shape,
        scratch,
        "backward",
        (16_000_000_000 * count, 20_000_000 * count, 0),
        tuple(args),
    )


def run_assemble_fc(start, mine, other):
    half = mine.shape[0]
    shapes = [(D, D), (D, FF), (FF, D), (D,), (D,), (D,), (FF,), (D,), (8, PAIR)]
    return kernel_call(
        assemble_fc_kernel,
        (1,),
        [whole((half, PAIR)), whole((half, PAIR))],
        [whole(size) for size in shapes],
        [shape_of(size, f32) for size in shapes],
        [],
        "assemble_fc",
        (10_000_000, 8_000_000, 0),
        (start, mine, other),
    )


def run_assemble_qkv(start, mine, other, norms, means):
    half = mine.shape[0]
    shapes = [(DIN, D), (D, 3 * D), (D,), (D,), (D,), (D,), (D,), (D,), (4,), (1,)]
    return kernel_call(
        assemble_qkv_kernel,
        (1,),
        [whole((half, PAIR)), whole((half, PAIR)), whole((8, PAIR)), whole((8, PAIR))],
        [whole(size) for size in shapes],
        [shape_of(size, f32) for size in shapes],
        [],
        "assemble_qkv",
        (10_000_000, 5_000_000, 0),
        (start, mine, other, norms, means),
    )


def add_received(kept, received):
    return kept.astype(f32) + received.astype(f32)


def shards(x_vis, vis_pos, *rest):
    params, cotangent = rest[:-1], rest[-1]
    w_proj, ln1_gain, w_qkv = params[0], params[3], params[5]
    seq_size = lax.axis_size("seq")
    clip_size = lax.axis_size("clip")
    groups = seq_size * clip_size // 2
    rows = LEN // seq_size
    clips, visible, _ = x_vis.shape
    members = [
        [s * clip_size + c for s in range(core, seq_size, 2) for c in range(clip_size)]
        for core in range(2)
    ]

    def chunk_rows(used):
        return -(-used // (32 * groups)) * 16

    core_pairs = [(s, s ^ 1) for s in range(seq_size)]
    chip_pairs = [(s, s ^ 2) for s in range(seq_size)]

    def across_core(value):
        return lax.ppermute(value, "seq", core_pairs)

    def swap(value):
        chunks = value.reshape(groups, -1, PAIR)
        return lax.all_to_all(chunks, AXES, 0, 0, axis_index_groups=members)

    def spread(chunks):
        total = jnp.sum(chunks.astype(f32), axis=0).astype(bf16)
        return jnp.broadcast_to(total[None], chunks.shape)

    fc_chunk = chunk_rows(FC_USED)
    qkv_chunk = chunk_rows(QKV_USED)
    qkv_half = qkv_chunk * groups
    seq_index = lax.axis_index("seq")
    bit = seq_index & 1
    first = seq_index * rows
    local_pos = jnp.where(vis_pos >= first, vis_pos - first, vis_pos - first + LEN)
    padded_pos = jnp.pad(local_pos, ((0, 0), (0, SLOT - visible)), constant_values=-1)
    table = sinusoid_table(LEN, D)
    table = jnp.asarray(np.concatenate([table, table[: LEN - rows]]).reshape(-1, 8, D))
    start = jnp.stack([first // 8, bit]).astype(jnp.int32)

    (
        output,
        grads,
        extra,
        gmid,
        kept,
        sent,
        norms,
        weights,
        query,
        key,
        value,
        normed,
        xhat,
        rstd,
    ) = run_forward(start, x_vis, local_pos, table, params, cotangent, rows, fc_chunk * groups)
    fc = add_received(kept, across_core(sent)).astype(bf16)
    fc, query = lax.optimization_barrier((fc, query))
    fc = swap(fc)
    saved = (query, key, value, grads, extra, weights, normed, xhat, rstd, gmid)
    acc, proj_kept0, proj_sent0 = run_backward(
        start, saved, x_vis, padded_pos, w_qkv, ln1_gain, rows, qkv_half, 0, clips - 1, None
    )
    fc, acc = lax.optimization_barrier((spread(fc), acc))
    fc = swap(fc).reshape(groups * fc_chunk, PAIR)
    kept, sent, proj_kept1, proj_sent1 = run_backward(
        start, saved, x_vis, padded_pos, w_qkv, ln1_gain, rows, qkv_half, clips - 1, 1, acc
    )
    qkv = add_received(kept, across_core(sent)).astype(bf16)
    fc, qkv = lax.optimization_barrier((fc, qkv))
    qkv = swap(qkv)
    w_out_g, w_fc1_g, w_fc2_g, b_out_g, gain2_g, bias2_g, b_fc1_g, b_fc2_g, means = (
        run_assemble_fc(start, fc, across_core(fc))
    )
    proj_kept = jnp.concatenate([proj_kept0, proj_kept1])
    proj_sent = jnp.concatenate([proj_sent0, proj_sent1])
    part = add_received(proj_kept, across_core(proj_sent)).astype(bf16)
    part = add_received(part, lax.ppermute(part, "seq", chip_pairs)).astype(bf16)
    qkv, means, part = lax.optimization_barrier((spread(qkv), means, part))
    qkv = swap(qkv).reshape(groups * qkv_chunk, PAIR)
    other = across_core(part)
    grad_projected = jnp.where(
        bit == 0,
        jnp.concatenate([part, other], axis=1),
        jnp.concatenate([other, part], axis=1),
    )[:, :visible]
    grad_x = lax.dot_general(
        grad_projected, w_proj, (((2,), (1,)), ((), ())), preferred_element_type=f32
    )
    (
        w_proj_g,
        w_qkv_g,
        b_proj_g,
        mask_g,
        gain1_g,
        bias1_g,
        q_bias_g,
        v_bias_g,
        trust,
        trust_qkv,
    ) = run_assemble_qkv(start, qkv, across_core(qkv), norms, means)
    return (
        output.reshape(clips, rows, D),
        grad_x,
        w_proj_g,
        b_proj_g,
        mask_g,
        gain1_g,
        bias1_g,
        w_qkv_g,
        q_bias_g,
        v_bias_g,
        w_out_g,
        b_out_g,
        gain2_g,
        bias2_g,
        w_fc1_g,
        b_fc1_g,
        w_fc2_g,
        b_fc2_g,
        trust,
        trust_qkv,
    )


def solution(mesh):
    return jax.shard_map(
        shards,
        mesh=mesh,
        in_specs=(P("clip", None, None), P("clip", None))
        + (P(),) * 16
        + (P("clip", "seq", None),),
        out_specs=(P("clip", "seq", None), P("clip", None, None)) + (P(),) * 18,
        check_vma=False,
    )
```

time: 266 us -> 234 us (0.88)
  other arithmetic: 37.8 us -> 9.61 us
  blocking collectives: 0 us -> 26 us
  starting transfers between devices: 47.2 us -> 26.4 us
  local copies, waits for them, and re-layouts: 13.4 us -> 4.88 us
  between operations: 9.02 us -> 0.96 us
  Pallas kernels: 142 us -> 148 us
    ppermute x23 -> x7, starting transfers between devices: 47.2 us -> 6.51 us  [the longest x6 4.86 us: across_core(): return lax.ppermute(value, 'seq', core_pairs)]
    all_to_all x0 -> x1, blocking collectives: none -> 26 us  [swap(): return lax.all_to_all(chunks, AXES, 0, 0, axis_index_groups=members)]
    all_to_all x0 -> x3, starting transfers between devices: none -> 19.9 us  [swap(): return lax.all_to_all(chunks, AXES, 0, 0, axis_index_groups=members)]
    reduce_sum x9 -> x2, other arithmetic: 15.6 us -> 0.3 us  [spread(): total = jnp.sum(chunks.astype(f32), axis=0).astype(bf16)]
    add x8 -> x0, other arithmetic: 6.69 us -> none  [sum_everywhere(): data = kept + lax.ppermute(sent, AXES, pairs).astype(f32)]
    convert_element_type x11 -> x0, local copies, waits for them, and re-layouts: 6.15 us -> none  [the longest x10 5.43 us: sum_everywhere(): lax.dynamic_slice_in_dim(data, (1 - bit) * half, half, 0).astype(bf16)]
    pallas_call x2 -> x5, Pallas kernels: 142 us -> 148 us  [kernel_call(): pl.pallas_call(kernel, grid_spec=pltpu.PrefetchScalarGridSpec(num_scalar_...]
    select_n x8 -> x0, other arithmetic: 5.75 us -> none  [sum_everywhere(): jnp.where(bit == 0, jnp.concatenate([data, other]), jnp.concatenate([othe...]
  transfers between devices with their start and end apart: 23 -> 10, of which waited for: 9 -> 6; matrix products, arithmetic and copies ran while one was open for 14% -> 3% of each run, Pallas kernels for 24% -> 31%
where the time goes in v2:
time: 234 us; the launch traced here: 233 us
  Pallas kernels  148 us (63%)
  starting transfers between devices  26.4 us (11%)
  blocking collectives  26 us (11%)
  waiting for transfers between devices  16.1 us (7%)
  other arithmetic  9.61 us (4%)
  local copies, waits for them, and re-layouts  4.88 us (2%)
    pallas_call x5, Pallas kernels, kernel_call(): pl.pallas_call(kernel, grid_spec=pltpu.PrefetchScalarGridSpec(num_scalar_...  148 us
    all_to_all x1, blocking collectives, swap(): return lax.all_to_all(chunks, AXES, 0, 0, axis_index_groups=members)  26 us
    all_to_all x3, starting transfers between devices, swap(): return lax.all_to_all(chunks, AXES, 0, 0, axis_index_groups=members)  19.9 us
    ppermute x6, waiting for transfers between devices, across_core(): return lax.ppermute(value, 'seq', core_pairs)  8.59 us
    ppermute x1, waiting for transfers between devices, shards(): lax.ppermute(part, 'seq', chip_pairs)  6.77 us
    ppermute x6, starting transfers between devices, across_core(): return lax.ppermute(value, 'seq', core_pairs)  4.86 us
  transfers between devices with their start and end apart: 10, of which 6 were waited for; matrix products, arithmetic and copies ran while one was open for 3% of the time, Pallas kernels for 31%

profile of v2, /device:TPU:1, one launch (start us, length us, event | category | flops | bytes accessed | tf_op | source)
XLA Modules:
  0.0 233.3 jit_solution(5731926861682006887)
XLA Ops:
  2.6 70.6 %forward.1 = (bf16[1176,384]{1,0:T(8,128)(2,1)}, bf16[1176,384]{1,0:T(8,128)(2,1)}, bf16[1176,128]{1,0:T(8,128)(2,1)}, f32[1176,384]{1,0:T(8,128)}, bf16[5376,12...) custom-call(s32[2]{0:T(128)} %pad_add_fusion.start_ref, ...), custom_call_target="tpu_custom_call" | custom-call | flops 40000000000 | bytes 60000000 | tf_op jit(solution)/shard_map/forward/pallas_call | solution.py:689
  74.2 2.4 %collective-permute-done = bf16[5376,128]{1,0:T(8,128)(2,1)S(1)} collective-permute-done((bf16[5376,128]{1,0:T(8,128)(2,1)}, bf16[5376,128]{1,0:T(8,128)(2,1)S(1)}, u32[]{:S(2)}, u32[]{:S(2)}) %collective-permute-start) | collective-permute-done | bytes 1376288 | tf_op jit(solution)/shard_map/ppermute | solution.py:990
  76.6 2.8 %add_convert_fusion = bf16[5376,128]{1,0:T(8,128)(2,1)} fusion(bf16[5376,128]{1,0:T(8,128)(2,1)S(1)} %collective-permute-done, bf16[5376,128]{1,0:T(8,128)(2,1)} %get-tuple-element.70), kind=kLoop, calls=%fused_computation | loop fusion | flops 2752512 | bytes 4128768 | tf_op jit(solution)/shard_map/convert_element_type | solution.py:1028
  79.4 7.7 %all-to-all-start = ((bf16[16,336,128]{2,1,0:T(8,128)(2,1)}), bf16[16,336,128]{2,1,0:T(8,128)(2,1)S(1)}, u32[]{:S(2)}, u32[]{:S(2)}) async-start(bf16[16,336,128]{2,1,0:T(8,128)(2,1)} %bitcast.4), calls=%async_computation | async-start | bytes 2752512 | tf_op jit(solution)/shard_map/all_to_all | solution.py:994
  87.1 42.7 %backward.2 = (f32[6144,128]{1,0:T(8,128)}, f32[2,80,384]{2,1,0:T(8,128)}, bf16[2,80,384]{2,1,0:T(8,128)(2,1)}) custom-call(s32[2]{0:T(128)} %pad_add_fusion.start_ref, bf16[3,392,384]{2,1,0:T(8,128)(2,1)} %get-tuple-element.74.q_ref, bf16[3,1568,384]{2,1,0:T(8,128)(2,1)} %get-tuple-element.75.k_ref, bf16[3,1568,384]{2,1,0:T(8,128)(2,1)} %get-tuple-element.76.v_ref, ...), custom_call_target="tpu_custom_call" | custom-call | flops 32000000000 | bytes 40000000 | tf_op jit(solution)/shard_map/backward/pallas_call | solution.py:689
  130.0 1.3 broadcast_in_dim.9
  131.2 6.3 %all-to-all-start.1 = ((bf16[16,336,128]{2,1,0:T(8,128)(2,1)}), bf16[16,336,128]{2,1,0:T(8,128)(2,1)S(1)}, u32[]{:S(2)}, u32[]{:S(2)}) async-start(bf16[16,336,128]{2,1,0:T(8,128)(2,1)} %broadcast_in_dim.9), calls=%async_computation.1 | async-start | bytes 2752512 | tf_op jit(solution)/shard_map/all_to_all | solution.py:994
  137.6 24.2 %backward.3 = (f32[3072,128]{1,0:T(8,128)}, bf16[3072,128]{1,0:T(8,128)(2,1)}, f32[1,80,384]{2,1,0:T(8,128)}, bf16[1,80,384]{2,1,0:T(8,128)(2,1)}) custom-call(s32[2]{0:T(128)} %pad_add_fusion.start_ref, bf16[3,392,384]{2,1,0:T(8,128)(2,1)} %get-tuple-element.74.q_ref, bf16[3,1568,384]{2,1,0:T(8,128)(2,1)} %get-tuple-element.75.k_ref, ...), custom_call_target="tpu_custom_call" | custom-call | flops 16000000000 | bytes 20000000 | tf_op jit(solution)/shard_map/backward/pallas_call | solution.py:689
  161.9 1.3 collective-permute-start.1
  163.1 2.1 collective-permute-done.1
  165.3 2.5 %add_convert_fusion.1 = bf16[3072,128]{1,0:T(8,128)(2,1)} fusion(f32[3072,128]{1,0:T(8,128)} %get-tuple-element.87, bf16[3072,128]{1,0:T(8,128)(2,1)S(1)} %collective-permute-done.1), kind=kLoop, calls=%fused_computation.1 | loop fusion | flops 1179648 | bytes 3145728 | tf_op jit(solution)/shard_map/convert_element_type | solution.py:1040
  168.5 5.9 %all-to-all-start.2 = ((bf16[16,192,128]{2,1,0:T(8,128)(2,1)}), bf16[16,192,128]{2,1,0:T(8,128)(2,1)S(1)}, u32[]{:S(2)}, u32[]{:S(2)}) async-start(bf16[16,192,128]{2,1,0:T(8,128)(2,1)} %bitcast.7), calls=%async_computation.2 | async-start | bytes 1572864 | tf_op jit(solution)/shard_map/all_to_all | solution.py:994
  175.1 1.0 pad_maximum_fusion.3
  176.1 2.0 collective-permute-done.3
  178.1 1.0 fusion.6
  179.2 1.6 collective-permute-start.4
  180.8 6.8 %collective-permute-done.4 = bf16[3,80,384]{2,1,0:T(8,128)(2,1)S(1)} collective-permute-done((bf16[3,80,384]{2,1,0:T(8,128)(2,1)S(1)}, bf16[3,80,384]{2,1,0:T(8,128)(2,1)S(1)}, u32[]{:S(2)}, u32[]{:S(2)}) %collective-permute-start.4) | collective-permute-done | bytes 184352 | tf_op jit(solution)/shard_map/ppermute | solution.py:1049
  188.3 1.1 copy-done.2
  189.4 5.8 %assemble_fc.1 = (f32[384,384]{1,0:T(8,128)}, f32[384,1536]{1,0:T(8,128)}, f32[1536,384]{1,0:T(8,128)}, f32[384]{0:T(512)}, f32[384]{0:T(512)}, /*index=5*/f32[3...) custom-call(s32[2]{0:T(128)} %pad_add_fusion.start_ref, bf16[5376,128]{1,0:T(8,128)(2,1)} %bitcast.14, ...), custom_call_target="tpu_custom_call" | custom-call | flops 10000000 | bytes 8000000 | tf_op jit(solution)/shard_map/assemble_fc/pallas_call | solution.py:689
  195.5 26.0 %all_to_all.20 = bf16[16,192,128]{2,1,0:T(8,128)(2,1)S(1)} all-to-all(bf16[16,192,128]{2,1,0:T(8,128)(2,1)S(1)} %broadcast_in_dim.22), channel_id=1, replica_groups={{0,1,2,3,4,5,6,7,16,17,18,19,20,21,22,23},{8,9,10,11,12,13,14,15,24,25,..., dimensions={0} | all-to-all | bytes 1572864 | tf_op jit(solution)/shard_map/all_to_all | solution.py:994
  221.5 2.6 %collective-permute-start.6 = (bf16[3072,128]{1,0:T(8,128)(2,1)S(1)}, bf16[3072,128]{1,0:T(8,128)(2,1)S(1)}, u32[]{:S(2)}, u32[]{:S(2)}) collective-permute-start(bf16[3072,128]{1,0:T(8,128)(2,1)S(1)} %bitcast.15), channel_id=1, source_target_pairs={{0,8},{8,0},{16,24},{24,16},{1,9},{9,1},{17,25},{25,17},{2,10},{10... | collective-permute-start | bytes 2359304 | tf_op jit(solution)/shard_map/ppermute | solution.py:990
  224.1 2.1 collective-permute-done.5
  226.2 1.7 fusion
  228.8 4.3 %assemble_qkv.1 = (f32[768,384]{1,0:T(8,128)}, f32[384,1152]{1,0:T(8,128)}, f32[384]{0:T(512)}, f32[384]{0:T(512)}, f32[384]{0:T(512)}, /*index=5*/f32[384]{0:T(...) custom-call(s32[2]{0:T(128)} %pad_add_fusion.start_ref, bf16[3072,128]{1,0:T(8,128)(2,1)} %bitcast.16, ...), custom_call_target="tpu_custom_call" | custom-call | flops 10000000 | bytes 5000000 | tf_op jit(solution)/shard_map/assemble_qkv/pallas_call | solution.py:689
  (29 shorter events, 6.7 us)
Async XLA Ops:
  73.2 3.4 %collective-permute-start = (bf16[5376,128]{1,0:T(8,128)(2,1)}, bf16[5376,128]{1,0:T(8,128)(2,1)S(1)}, u32[]{:S(2)}, u32[]{:S(2)}) collective-permute-start(bf16[5376,128]{1,0:T(8,128)(2,1)} %get-tuple-element.71), channel_id=1, source_target_pairs={{0,8},{8,0},{16,24},{24,16},{1,9},{9,1},{17,25},{25,17},{2,10},{10... | collective-permute-start | bytes 4128776 | tf_op jit(solution)/shard_map/ppermute | solution.py:990
  79.4 50.4 %all-to-all-start = ((bf16[16,336,128]{2,1,0:T(8,128)(2,1)}), bf16[16,336,128]{2,1,0:T(8,128)(2,1)S(1)}, u32[]{:S(2)}, u32[]{:S(2)}) async-start(bf16[16,336,128]{2,1,0:T(8,128)(2,1)} %bitcast.4), calls=%async_computation | async-start | bytes 2752512 | tf_op jit(solution)/shard_map/all_to_all | solution.py:994
  131.2 37.3 %all-to-all-start.1 = ((bf16[16,336,128]{2,1,0:T(8,128)(2,1)}), bf16[16,336,128]{2,1,0:T(8,128)(2,1)S(1)}, u32[]{:S(2)}, u32[]{:S(2)}) async-start(bf16[16,336,128]{2,1,0:T(8,128)(2,1)} %broadcast_in_dim.9), calls=%async_computation.1 | async-start | bytes 2752512 | tf_op jit(solution)/shard_map/all_to_all | solution.py:994
  161.9 3.4 %collective-permute-start.1 = (bf16[3072,128]{1,0:T(8,128)(2,1)}, bf16[3072,128]{1,0:T(8,128)(2,1)S(1)}, u32[]{:S(2)}, u32[]{:S(2)}) collective-permute-start(bf16[3072,128]{1,0:T(8,128)(2,1)} %get-tuple-element.88), channel_id=1, source_target_pairs={{0,8},{8,0},{16,24},{24,16},{1,9},{9,1},{17,25},{25,17},{2,10},{10... | collective-permute-start | bytes 2359304 | tf_op jit(solution)/shard_map/ppermute | solution.py:990
  168.5 19.8 %copy-start = (bf16[16,336,128]{2,1,0:T(8,128)(2,1)}, bf16[16,336,128]{2,1,0:T(8,128)(2,1)S(1)}, u32[]{:S(2)}) copy-start(bf16[16,336,128]{2,1,0:T(8,128)(2,1)S(1)} %all-to-all-done.1) | copy-start | bytes 4128772
  168.5 26.7 %all-to-all-start.2 = ((bf16[16,192,128]{2,1,0:T(8,128)(2,1)}), bf16[16,192,128]{2,1,0:T(8,128)(2,1)S(1)}, u32[]{:S(2)}, u32[]{:S(2)}) async-start(bf16[16,192,128]{2,1,0:T(8,128)(2,1)} %bitcast.7), calls=%async_computation.2 | async-start | bytes 1572864 | tf_op jit(solution)/shard_map/all_to_all | solution.py:994
  174.4 13.9 %collective-permute-start.2 = (bf16[5376,128]{1,0:T(8,128)(2,1)S(1)}, bf16[5376,128]{1,0:T(8,128)(2,1)S(1)}, u32[]{:S(2)}, u32[]{:S(2)}) collective-permute-start(bf16[5376,128]{1,0:T(8,128)(2,1)S(1)} %bitcast.13), channel_id=1, source_target_pairs={{0,8},{8,0},{16,24},{24,16},{1,9},{9,1},{17,25},{25,17},{2,10},{10... | collective-permute-start | bytes 4128776 | tf_op jit(solution)/shard_map/ppermute | solution.py:990
  176.1 2.1 collective-permute-start.3
  179.2 8.4 %collective-permute-start.4 = (bf16[3,80,384]{2,1,0:T(8,128)(2,1)S(1)}, bf16[3,80,384]{2,1,0:T(8,128)(2,1)S(1)}, u32[]{:S(2)}, u32[]{:S(2)}) collective-permute-start(bf16[3,80,384]{2,1,0:T(8,128)(2,1)S(1)} %fusion.6), channel_id=1, source_target_pairs={{0,16},{8,24},{16,0},{24,8},{1,17},{9,25},{17,1},{25,9},{2,18},{10... | collective-permute-start | bytes 552968 | tf_op jit(solution)/shard_map/ppermute | solution.py:1049
  188.3 1.1 copy-start.2
  195.2 28.9 %copy-start.4 = (bf16[3,80,384]{2,1,0:T(8,128)(2,1)S(1)}, bf16[3,80,384]{2,1,0:T(8,128)(2,1)}, u32[]{:S(2)}) copy-start(bf16[3,80,384]{2,1,0:T(8,128)(2,1)} %add_convert_fusion.2) | copy-start | bytes 552964
  195.2 31.0 %copy-start.5 = (bf16[768,384]{1,0:T(8,128)(2,1)S(1)}, bf16[768,384]{1,0:T(8,128)(2,1)}, u32[]{:S(2)}) copy-start(bf16[768,384]{1,0:T(8,128)(2,1)} %w_proj_ref.1) | copy-start | bytes 1769476
  221.5 6.5 %copy-start.1 = (bf16[16,192,128]{2,1,0:T(8,128)(2,1)}, bf16[16,192,128]{2,1,0:T(8,128)(2,1)S(1)}, u32[]{:S(2)}) copy-start(bf16[16,192,128]{2,1,0:T(8,128)(2,1)S(1)} %all_to_all.20) | copy-start | bytes 2359300
  221.5 6.5 %collective-permute-start.6 = (bf16[3072,128]{1,0:T(8,128)(2,1)S(1)}, bf16[3072,128]{1,0:T(8,128)(2,1)S(1)}, u32[]{:S(2)}, u32[]{:S(2)}) collective-permute-start(bf16[3072,128]{1,0:T(8,128)(2,1)S(1)} %bitcast.15), channel_id=1, source_target_pairs={{0,8},{8,0},{16,24},{24,16},{1,9},{9,1},{17,25},{25,17},{2,10},{10... | collective-permute-start | bytes 2359304 | tf_op jit(solution)/shard_map/ppermute | solution.py:990
  224.1 2.2 collective-permute-start.5
  227.9 0.9 copy-start.3
